TPU v7x, 32 devices: a whole 2x2x4 slice. The times are simulated.
32 devices in a mesh: groups: 2 (over x), expert: 16 (over z, y, core).
Axes of the slice: x: 2, y: 2, z: 4, core: 2. Of those that a mesh axis runs over, the one named last changes fastest.
Arguments:
- tokens: bfloat16 [512, 2048], P(('groups', 'expert')), parts along dimension 0, may hold values from -6 to 6
- depths: int32 [512], P(('groups', 'expert')), parts along dimension 0, may hold values from 1 to 2
- routes: int32 [2, 512, 8], P(None, ('groups', 'expert')), parts along dimension 1, may hold values from 0 to 15, all different within a row; in each aligned block of 16 rows (0 to 15, 16 to 31, ..., all dimensions but the last counted through in order) at most 16 rows name the same one
- norm_gain: bfloat16 [2048], replicated, may hold values from 0.099609375 to 1.8984375
- router: bfloat16 [2048, 16], replicated, may hold values from -0.125 to 0.125
- w_gate: bfloat16 [16, 2048, 768], P('expert'), may hold values from -0.125 to 0.125
- w_up: bfloat16 [16, 2048, 768], P('expert'), may hold values from -0.125 to 0.125
- w_down: bfloat16 [16, 768, 2048], P('expert'), may hold values from -0.21875 to 0.21875
- replica_plan: int32 [16], replicated, may hold values from 0 to 15, as said below
- copy_choice: int32 [16, 16], P('expert'), may hold values from 0 to 15, as said below
Outputs:
- final_state: bfloat16 [512, 2048], P(('groups', 'expert')), parts along dimension 0
- copy_load: float32 [32, 4], P(('groups', 'expert')), parts along dimension 0
There are 2 independent parts, one for each index of `groups`. A program takes and returns all parts, laid end to end along the dimension named above; an argument that names none is the same for every part. Nothing has to cross between parts.
Inputs may be any that keep to these rules, and one draw needn't show every extreme that they name: `routes`: in each pass the 8 experts of a row differ, and no expert is named by more than 16 rows of one device (an aligned block of 16 rows); some expert is named by exactly 16 rows in some blocks. replica_plan[d] is never d. copy_choice[s, e] is a device number.
All inputs are finite; a program needn't handle non-finite values.
Results may differ from a plain program's by a relative error of at most 0.0038.
The roundings to bfloat16 on the way count: a program that leaves them out, or rounds other values in their place, can miss the bound.
Values may be sent and summed in bfloat16 or wider, within the bound.
No kernel may reach another device: no remote copies, remote signals or barrier semaphores. Data moves between devices by JAX's collectives and lax.ppermute only.
A program may use at most 64 MiB of HBM per device.

v0:
```python
import jax
import jax.numpy as jnp
from jax import lax
from jax.sharding import PartitionSpec as P


def expert_ffn(rows_in, gate_w, up_w, down_w):
    gate_val = jnp.dot(rows_in, gate_w, preferred_element_type=jnp.float32)
    up_val = jnp.dot(rows_in, up_w, preferred_element_type=jnp.float32)
    hidden = (jax.nn.silu(gate_val) * up_val).astype(jnp.bfloat16)
    return jnp.dot(hidden, down_w, preferred_element_type=jnp.float32).astype(jnp.bfloat16)


def body(
    tokens, depths, routes, norm_gain, router, w_gate, w_up, w_down, replica_plan, copy_choice
):
    highest = lax.Precision.HIGHEST
    peer_count = lax.axis_size("expert")
    row_count, model_width = tokens.shape
    iter_count, _, top_count = routes.shape
    cap_rows = 2 * row_count * top_count // peer_count
    expert_ids = jnp.arange(peer_count, dtype=jnp.int32)
    copy_row = copy_choice[0]
    home_gate, home_up, home_down = (w_gate[0], w_up[0], w_down[0])
    onehot_all = routes[:, :, :, None] == expert_ids
    wanted_all = jnp.sum(jnp.where(onehot_all, copy_row, 0), axis=3)
    plan_at = jnp.sum(jnp.where(wanted_all[..., None] == expert_ids, replica_plan, 0), axis=3)
    valid_all = (plan_at == routes) & (wanted_all != routes)
    target_all = jnp.where(valid_all, wanted_all, routes)
    slot_all = valid_all.astype(jnp.int32)
    active_all = depths[None, :] > jnp.arange(iter_count, dtype=jnp.int32)[:, None]
    live_all = jnp.broadcast_to(active_all[:, :, None], routes.shape)
    bucket_all = target_all * 2 + slot_all
    bucket_hot = (bucket_all[..., None] == jnp.arange(2 * peer_count, dtype=jnp.int32)) & live_all[
        ..., None
    ]
    counts = jnp.sum(bucket_hot.astype(jnp.float32), axis=(1, 2)).reshape(iter_count, peer_count, 2)
    counts = jnp.transpose(counts, (1, 0, 2)).reshape(peer_count, 2 * iter_count)
    copy_load = lax.psum_scatter(counts, "expert", scatter_dimension=0, tiled=True) / float(
        row_count * top_count
    )
    slot_count = 1
    pair_rows = jnp.repeat(jnp.arange(row_count, dtype=jnp.int32), top_count)
    buffer_rows = peer_count * cap_rows * slot_count
    state = tokens
    for layer_step in range(iter_count):
        state32 = state.astype(jnp.float32)
        scale = lax.rsqrt(jnp.mean(state32 * state32, axis=1, keepdims=True) + 1e-06)
        normed = (state32 * scale * norm_gain.astype(jnp.float32)).astype(jnp.bfloat16)
        logits = jnp.dot(normed, router, preferred_element_type=jnp.float32)
        picked = jnp.sum(jnp.where(onehot_all[layer_step], logits[:, None, :], 0.0), axis=2)
        sigmas = jax.nn.sigmoid(picked)
        gates = sigmas / jnp.sum(sigmas, axis=1, keepdims=True)
        target_dev = routes[layer_step]
        live_pairs = live_all[layer_step].reshape(-1)
        bucket = (target_dev * slot_count).reshape(-1)
        bucket_flags = (
            (bucket[:, None] == jnp.arange(peer_count * slot_count, dtype=jnp.int32))
            & live_pairs[:, None]
        ).astype(jnp.int32)
        rank_table = jnp.cumsum(bucket_flags, axis=0)
        position = jnp.sum(rank_table * bucket_flags, axis=1) - 1
        index_flat = (target_dev.reshape(-1) * cap_rows + position) * slot_count
        send_index = jnp.where(live_pairs, index_flat, buffer_rows)
        outbound = (
            jnp.zeros((buffer_rows, model_width), jnp.bfloat16)
            .at[send_index]
            .set(normed[pair_rows], mode="drop")
        )
        outbound = outbound.reshape(peer_count, cap_rows, slot_count, model_width)
        received = lax.all_to_all(outbound, "expert", split_axis=0, concat_axis=0, tiled=True)
        count = received.shape[1]
        first_rows = received[:, :, 0, :].reshape(peer_count * count, model_width)
        result = expert_ffn(first_rows, home_gate, home_up, home_down).reshape(
            peer_count, count, 1, model_width
        )
        returned = lax.all_to_all(result, "expert", split_axis=0, concat_axis=0, tiled=True)
        read_index = jnp.where(live_pairs, index_flat, 0)
        pair_out = returned.reshape(buffer_rows, model_width)[read_index].reshape(
            row_count, top_count, model_width
        )
        weights = gates * live_all[layer_step].astype(jnp.float32)
        delta = jnp.einsum("rk,rkd->rd", weights, pair_out.astype(jnp.float32), precision=highest)
        state = (state32 + delta).astype(jnp.bfloat16)
    return (state, copy_load)


def solution(mesh):
    return jax.shard_map(
        body,
        mesh=mesh,
        in_specs=(
            P(("groups", "expert"), None),
            P(("groups", "expert")),
            P(None, ("groups", "expert"), None),
            P(),
            P(),
            P("expert", None, None),
            P("expert", None, None),
            P("expert", None, None),
            P(),
            P("expert", None),
        ),
        out_specs=(P(("groups", "expert"), None), P(("groups", "expert"), None)),
        check_vma=False,
    )
```

profile of v0, /device:TPU:0, one launch (start us, length us, event | category | flops | bytes accessed | tf_op | source)
XLA Modules:
  0.0 190.1 jit_solution(3896953000903324033)
XLA Ops:
  0.6 0.8 iota_compare_fusion.5
  1.7 1.0 fusion.46
  2.7 0.7 convert_element_type.51
  3.5 0.7 fusion.67
  5.0 0.9 fusion.48
  6.0 4.1 %scatter_custom_fusion = bf16[256,2048]{1,0:T(8,128)(2,1)} fusion(s32[128]{0:T(128)S(1)} %get-tuple-element.19, bf16[16,2048]{1,0:T(8,128)(2,1)S(1)} %fusion.48, s32[1024]{0:T(1024)S(1)} %pad_clamp_fusion.2, bf16[]{:T(256)} %constant.33.clone.1), kind=kCustom, calls=%fused_computation.30 | custom fusion | bytes 1048578 | tf_op jit(solution)/shard_map/scatter | solution.py:68
  10.1 32.1 %all_to_all.20 = bf16[16,16,1,2048]{3,1,2,0:T(8,128)(2,1)S(1)} all-to-all(bf16[16,16,1,2048]{3,1,2,0:T(8,128)(2,1)} %bitcast.113), channel_id=1, replica_groups=mesh['groups'=2,'expert'=16] {'expert'}, dimensions={0} | all-to-all | bytes 2097152 | tf_op jit(solution)/shard_map/all_to_all | solution.py:71
  42.2 1.0 copy-done.1
  43.2 3.8 %fusion.10 = f32[256,768]{1,0:T(8,128)} fusion(bf16[256,2048]{1,0:T(8,128)(2,1)S(1)} %bitcast.116, bf16[1,2048,768]{2,1,0:T(8,128)(2,1)} %param.15), kind=kOutput, calls=%fused_computation.16 | convolution fusion | flops 805306368 | bytes 4980736 | tf_op jit(solution)/shard_map/dot_general | solution.py:8
  47.0 5.5 %fusion.12 = bf16[256,2048]{1,0:T(8,128)(2,1)} fusion(bf16[1,768,2048]{2,1,0:T(8,128)(2,1)S(1)} %copy-done, bf16[256,2048]{1,0:T(8,128)(2,1)} %bitcast.117, bf16[1,2048,768]{2,1,0:T(8,128)(2,1)} %param.16, f32[256,768]{1,0:T(8,128)} %fusion.10), kind=kOutput, calls=%fused_computation.18 | convolution fusion | flops 1612316672 | bytes 9175040 | tf_op jit(solution)/shard_map/dot_general | solution.py:11
  52.6 5.1 %all-to-all-start.1 = ((bf16[16,16,1,2048]{3,1,2,0:T(8,128)(2,1)}), bf16[16,16,1,2048]{3,1,2,0:T(8,128)(2,1)}, u32[]{:S(2)}, u32[]{:S(2)}) async-start(bf16[16,16,1,2048]{3,1,2,0:T(8,128)(2,1)} %bitcast.115), calls=%async_computation.1 | async-start | bytes 2097152 | tf_op jit(solution)/shard_map/all_to_all | solution.py:77
  59.4 21.2 %all-to-all-done.1 = bf16[16,16,1,2048]{3,1,2,0:T(8,128)(2,1)} async-done(((bf16[16,16,1,2048]{3,1,2,0:T(8,128)(2,1)}), bf16[16,16,1,2048]{3,1,2,0:T(8,128)(2,1)}, u32[]{:S(2)}, u32[]{:S(2)}) %all-to-all-start.1) | async-done | bytes 1048608 | tf_op jit(solution)/shard_map/all_to_all | solution.py:77
  80.6 3.6 %gather_fusion = bf16[128,2048]{1,0:T(8,128)(2,1)} fusion(bf16[256,2048]{1,0:T(8,128)(2,1)} %bitcast.14, s32[1024]{0:T(1024)S(1)} %pad_clamp_fusion.1), kind=kCustom, calls=%fused_computation.1 | custom fusion | bytes 1049088 | tf_op jit(solution)/shard_map/gather | solution.py:79
  84.2 1.6 fusion.36
  86.0 4.1 %scatter_custom_fusion.1 = bf16[256,2048]{1,0:T(8,128)(2,1)} fusion(s32[128]{0:T(128)S(1)} %get-tuple-element.17, bf16[16,2048]{1,0:T(8,128)(2,1)S(1)} %fusion.52, s32[1024]{0:T(1024)S(1)} %pad_clamp_fusion.2, bf16[]{:T(256)} %constant.33.clone.1), kind=kCustom, calls=%fused_computation.28 | custom fusion | bytes 1048578 | tf_op jit(solution)/shard_map/scatter | solution.py:68
  90.2 31.5 %all_to_all.21 = bf16[16,16,1,2048]{3,1,2,0:T(8,128)(2,1)S(1)} all-to-all(bf16[16,16,1,2048]{3,1,2,0:T(8,128)(2,1)} %bitcast.112), channel_id=1, replica_groups=mesh['groups'=2,'expert'=16] {'expert'}, dimensions={0} | all-to-all | bytes 2097152 | tf_op jit(solution)/shard_map/all_to_all | solution.py:71
  121.6 1.0 copy-done.2
  122.7 3.8 %fusion.8 = f32[256,768]{1,0:T(8,128)} fusion(bf16[256,2048]{1,0:T(8,128)(2,1)S(1)} %bitcast.118, bf16[1,2048,768]{2,1,0:T(8,128)(2,1)} %param.15), kind=kOutput, calls=%fused_computation.14 | convolution fusion | flops 805306368 | bytes 4980736 | tf_op jit(solution)/shard_map/dot_general | solution.py:8
  126.4 5.5 %fusion.15 = bf16[256,2048]{1,0:T(8,128)(2,1)} fusion(bf16[1,768,2048]{2,1,0:T(8,128)(2,1)S(1)} %copy-done, bf16[256,2048]{1,0:T(8,128)(2,1)} %bitcast.119, bf16[1,2048,768]{2,1,0:T(8,128)(2,1)} %param.16, f32[256,768]{1,0:T(8,128)} %fusion.8), kind=kOutput, calls=%fused_computation.19 | convolution fusion | flops 1612316672 | bytes 9175040 | tf_op jit(solution)/shard_map/dot_general | solution.py:11
  132.0 5.1 %all-to-all-start.3 = ((bf16[16,16,1,2048]{3,1,2,0:T(8,128)(2,1)}), bf16[16,16,1,2048]{3,1,2,0:T(8,128)(2,1)}, u32[]{:S(2)}, u32[]{:S(2)}) async-start(bf16[16,16,1,2048]{3,1,2,0:T(8,128)(2,1)} %bitcast.114), calls=%async_computation.3 | async-start | bytes 2097152 | tf_op jit(solution)/shard_map/all_to_all | solution.py:77
  139.4 43.0 %all-reduce = f32[16,4]{0,1:T(4,128)S(1)} all-reduce(f32[16,4]{0,1:T(4,128)S(1)} %bitcast.123), channel_id=2, replica_groups=mesh['groups'=2,'expert'=16] {'expert'}, use_global_device_ids=true, to_apply=%region_15.16.clone | all-reduce | flops 64 | bytes 512
  182.4 0.7 dynamic-slice_multiply_fusion
  184.2 3.6 %gather_fusion.1 = bf16[128,2048]{1,0:T(8,128)(2,1)} fusion(bf16[256,2048]{1,0:T(8,128)(2,1)} %bitcast.28, s32[1024]{0:T(1024)S(1)} %pad_clamp_fusion), kind=kCustom, calls=%fused_computation.3 | custom fusion | bytes 1049088 | tf_op jit(solution)/shard_map/gather | solution.py:79
  187.8 1.6 fusion.34
  (69 shorter events, 7.1 us)
Async XLA Ops:
  0.6 46.4 %copy-start = (bf16[1,768,2048]{2,1,0:T(8,128)(2,1)S(1)}, bf16[1,768,2048]{2,1,0:T(8,128)(2,1)}, u32[]{:S(2)}) copy-start(bf16[1,768,2048]{2,1,0:T(8,128)(2,1)} %param.17) | copy-start | bytes 9437188
  42.2 1.0 copy-start.1
  47.0 10.9 %copy-start.5 = (s32[2,16,8]{1,2,0:T(8,128)S(1)}, s32[2,16,8]{1,2,0:T(8,128)}, u32[]{:S(2)}) copy-start(s32[2,16,8]{1,2,0:T(8,128)} %param.12) | copy-start | bytes 3076
  47.0 11.7 %copy-start.4 = (bf16[2048,16]{0,1:T(8,128)(2,1)S(1)}, bf16[2048,16]{0,1:T(8,128)(2,1)}, u32[]{:S(2)}) copy-start(bf16[2048,16]{0,1:T(8,128)(2,1)} %param.14) | copy-start | bytes 196612
  52.6 28.0 %all-to-all-start.1 = ((bf16[16,16,1,2048]{3,1,2,0:T(8,128)(2,1)}), bf16[16,16,1,2048]{3,1,2,0:T(8,128)(2,1)}, u32[]{:S(2)}, u32[]{:S(2)}) async-start(bf16[16,16,1,2048]{3,1,2,0:T(8,128)(2,1)} %bitcast.115), calls=%async_computation.1 | async-start | bytes 2097152 | tf_op jit(solution)/shard_map/all_to_all | solution.py:77
  57.6 28.1 %copy-start.3 = (bf16[16,2048]{1,0:T(8,128)(2,1)S(1)}, bf16[16,2048]{1,0:T(8,128)(2,1)}, u32[]{:S(2)}) copy-start(bf16[16,2048]{1,0:T(8,128)(2,1)} %param.10) | copy-start | bytes 196612
  121.6 1.0 copy-start.2
  126.4 10.7 %copy-start.6 = (s32[1,16]{1,0:T(1,128)S(1)}, s32[1,16]{1,0:T(1,128)}, u32[]{:S(2)}) copy-start(s32[1,16]{1,0:T(1,128)} %param.19) | copy-start | bytes 196
  126.4 11.3 %copy-start.7 = (s32[16]{0:T(128)S(1)}, s32[16]{0:T(128)}, u32[]{:S(2)}) copy-start(s32[16]{0:T(128)} %param.18) | copy-start | bytes 196
  126.4 12.4 %copy-start.8 = (u32[32]{0:T(128)S(1)}, u32[32]{0:T(128)}, u32[]{:S(2)}) copy-start(u32[32]{0:T(128)} %constant.49) | copy-start | bytes 388
  132.0 52.2 %all-to-all-start.3 = ((bf16[16,16,1,2048]{3,1,2,0:T(8,128)(2,1)}), bf16[16,16,1,2048]{3,1,2,0:T(8,128)(2,1)}, u32[]{:S(2)}, u32[]{:S(2)}) async-start(bf16[16,16,1,2048]{3,1,2,0:T(8,128)(2,1)} %bitcast.114), calls=%async_computation.3 | async-start | bytes 2097152 | tf_op jit(solution)/shard_map/all_to_all | solution.py:77
where the time goes:
time: 191 us; the launch traced here: 190 us
  blocking collectives  107 us (56%)
  matrix products  22.1 us (12%)
  waiting for transfers between devices  21.2 us (11%)
  local copies, waits for them, and re-layouts  20.2 us (11%)
  starting transfers between devices  10.2 us (5%)
  other arithmetic  8.94 us (5%)
    all_to_all x2, blocking collectives, body(): lax.all_to_all(outbound, 'expert', split_axis=0, concat_axis=0, tiled=True)  63.6 us
    unnamed x1, blocking collectives  43 us
    all_to_all x2, waiting for transfers between devices, body(): lax.all_to_all(result, 'expert', split_axis=0, concat_axis=0, tiled=True)  21.2 us
    dot_general x2, matrix products, expert_ffn(): jnp.dot(hidden, down_w, preferred_element_type=jnp.float32)  11.1 us
    all_to_all x2, starting transfers between devices, body(): lax.all_to_all(result, 'expert', split_axis=0, concat_axis=0, tiled=True)  10.2 us
    scatter x2, local copies, waits for them, and re-layouts, body(): outbound = jnp.zeros((buffer_rows, model_width), jnp.bfloat16).at[send_in...  8.22 us
    dot_general x2, matrix products, expert_ffn(): gate_val = jnp.dot(rows_in, gate_w, preferred_element_type=jnp.float32)  7.55 us
    gather x2, local copies, waits for them, and re-layouts, body(): returned.reshape(buffer_rows, model_width)[read_index]  7.18 us
  transfers between devices with their start and end apart: 2, of which 1 were waited for; matrix products, arithmetic and copies ran while one was open for 3% of the time, Pallas kernels for 0%

commit v1 on v0

--- a/solution.py
+++ b/solution.py
@@ -1,7 +1,15 @@
+import functools
+
 import jax
 import jax.numpy as jnp
 from jax import lax
+from jax.experimental import pallas as pl
+from jax.experimental.pallas import tpu as pltpu
 from jax.sharding import PartitionSpec as P
+
+LANES = 128
+BF16 = jnp.bfloat16
+F32 = jnp.float32
 
 
 def expert_ffn(rows_in, gate_w, up_w, down_w):
@@ -11,7 +19,7 @@
     return jnp.dot(hidden, down_w, preferred_element_type=jnp.float32).astype(jnp.bfloat16)
 
 
-def body(
+def sparse_body(
     tokens, depths, routes, norm_gain, router, w_gate, w_up, w_down, replica_plan, copy_choice
 ):
     highest = lax.Precision.HIGHEST
@@ -39,9 +47,8 @@
     copy_load = lax.psum_scatter(counts, "expert", scatter_dimension=0, tiled=True) / float(
         row_count * top_count
     )
-    slot_count = 1
     pair_rows = jnp.repeat(jnp.arange(row_count, dtype=jnp.int32), top_count)
-    buffer_rows = peer_count * cap_rows * slot_count
+    buffer_rows = peer_count * cap_rows
     state = tokens
     for layer_step in range(iter_count):
         state32 = state.astype(jnp.float32)
@@ -53,27 +60,23 @@
         gates = sigmas / jnp.sum(sigmas, axis=1, keepdims=True)
         target_dev = routes[layer_step]
         live_pairs = live_all[layer_step].reshape(-1)
-        bucket = (target_dev * slot_count).reshape(-1)
+        bucket = target_dev.reshape(-1)
         bucket_flags = (
-            (bucket[:, None] == jnp.arange(peer_count * slot_count, dtype=jnp.int32))
-            & live_pairs[:, None]
+            (bucket[:, None] == jnp.arange(peer_count, dtype=jnp.int32)) & live_pairs[:, None]
         ).astype(jnp.int32)
         rank_table = jnp.cumsum(bucket_flags, axis=0)
         position = jnp.sum(rank_table * bucket_flags, axis=1) - 1
-        index_flat = (target_dev.reshape(-1) * cap_rows + position) * slot_count
+        index_flat = target_dev.reshape(-1) * cap_rows + position
         send_index = jnp.where(live_pairs, index_flat, buffer_rows)
         outbound = (
             jnp.zeros((buffer_rows, model_width), jnp.bfloat16)
             .at[send_index]
             .set(normed[pair_rows], mode="drop")
         )
-        outbound = outbound.reshape(peer_count, cap_rows, slot_count, model_width)
+        outbound = outbound.reshape(peer_count, cap_rows, 1, model_width)
         received = lax.all_to_all(outbound, "expert", split_axis=0, concat_axis=0, tiled=True)
-        count = received.shape[1]
-        first_rows = received[:, :, 0, :].reshape(peer_count * count, model_width)
-        result = expert_ffn(first_rows, home_gate, home_up, home_down).reshape(
-            peer_count, count, 1, model_width
-        )
+        first_rows = received.reshape(buffer_rows, model_width)
+        result = expert_ffn(first_rows, home_gate, home_up, home_down).reshape(outbound.shape)
         returned = lax.all_to_all(result, "expert", split_axis=0, concat_axis=0, tiled=True)
         read_index = jnp.where(live_pairs, index_flat, 0)
         pair_out = returned.reshape(buffer_rows, model_width)[read_index].reshape(
@@ -83,6 +86,150 @@
         delta = jnp.einsum("rk,rkd->rd", weights, pair_out.astype(jnp.float32), precision=highest)
         state = (state32 + delta).astype(jnp.bfloat16)
     return (state, copy_load)
+
+
+def ffn_kernel(step, x_ref, meta_ref, router_ref, gate_ref, up_ref, down_ref, own_ref, other_ref,
+               hidden_ref):
+    rows, width = x_ref.shape
+    top = 8
+    ff = gate_ref.shape[-1]
+    experts = router_ref.shape[1]
+    me = lax.axis_index("expert")
+    x = x_ref[...]
+    logits = jnp.dot(x, router_ref[...], preferred_element_type=F32)
+    sig = jax.nn.sigmoid(logits)
+    meta = meta_ref[...].astype(F32)
+    ids = lax.broadcasted_iota(jnp.int32, (rows, experts), 1)
+    idf = ids.astype(F32)
+    named = jnp.zeros((rows, experts), F32)
+    for k in range(top):
+        c = step * top + k
+        named = jnp.where(meta[:, c:c + 1] == idf, 1.0, named)
+    sig = jnp.where(named > 0.0, sig, 0.0)
+    total = jnp.sum(sig, axis=1, keepdims=True)
+    mine = jnp.sum(jnp.where(ids == me, sig, 0.0), axis=1, keepdims=True)
+    depth = meta[:, 2 * top:2 * top + 1]
+    weight = jnp.where(depth > float(step), mine / total, 0.0)
+
+    tile = 256
+
+    @pl.loop(0, ff // tile)
+    def _(i):
+        cols = pl.ds(pl.multiple_of(i * tile, tile), tile)
+        g = jnp.dot(x_ref[...], gate_ref[0, :, cols], preferred_element_type=F32)
+        u = jnp.dot(x_ref[...], up_ref[0, :, cols], preferred_element_type=F32)
+        hidden_ref[:, cols] = (g * jax.nn.sigmoid(g) * u).astype(BF16)
+
+    half = rows // 2
+
+    @pl.loop(0, width // tile)
+    def _(i):
+        cols = pl.ds(pl.multiple_of(i * tile, tile), tile)
+        o = jnp.dot(hidden_ref[...], down_ref[0, :, cols], preferred_element_type=F32)
+        o = o.astype(BF16).astype(F32) * weight
+        own_ref[:, cols] = o[:half].astype(BF16)
+        other_ref[:, cols] = o[half:].astype(BF16)
+
+
+def run_ffn(step, x, meta, router, w_gate, w_up, w_down):
+    rows, width = x.shape
+    ff = w_gate.shape[-1]
+    half = jax.ShapeDtypeStruct((rows // 2, width), BF16)
+    return pl.pallas_call(
+        functools.partial(ffn_kernel, step),
+        out_shape=(half, half),
+        in_specs=[pl.BlockSpec(memory_space=pltpu.VMEM)] * 6,
+        out_specs=(pl.BlockSpec(memory_space=pltpu.VMEM),) * 2,
+        scratch_shapes=[pltpu.VMEM((rows, ff), BF16)],
+        cost_estimate=pl.CostEstimate(
+            flops=6 * rows * width * ff, bytes_accessed=6 * width * ff, transcendentals=rows * ff
+        ),
+        name=f"ffn{step}",
+    )(x, meta, router, w_gate, w_up, w_down)
+
+
+def dense_body(
+    tokens, depths, routes, norm_gain, router, w_gate, w_up, w_down, replica_plan, copy_choice
+):
+    n = lax.axis_size("expert")
+    rows, width = tokens.shape
+    iters, _, top = routes.shape
+    chips = n // 2
+    ny = 1
+    while (2 * ny) * (2 * ny) <= chips:
+        ny *= 2
+    nz = chips // ny
+    zs = 2 * ny
+
+    def swap(x, offset):
+        return lax.ppermute(x, "expert", [(i, i ^ offset) for i in range(n)])
+
+    def gather(x):
+        zb = [x] + [swap(x, a * zs) for a in range(1, nz)]
+        z_all = jnp.concatenate(zb, 0)
+        plane = jnp.concatenate([z_all] + [swap(z_all, b * 2) for b in range(1, ny)], 0)
+        return jnp.concatenate([plane, swap(plane, 1)], 0)
+
+    def scatter(own, other):
+        plane = own.astype(F32) + swap(other, 1).astype(F32)
+        r = rows * nz
+        acc = plane[:r]
+        for b in range(1, ny):
+            acc = acc + swap(plane[b * r:(b + 1) * r].astype(BF16), b * 2).astype(F32)
+        out = acc[:rows]
+        for a in range(1, nz):
+            out = out + swap(acc[a * rows:(a + 1) * rows].astype(BF16), a * zs).astype(F32)
+        return out
+
+    pieces = [routes[t] for t in range(iters)] + [
+        depths[:, None],
+        jnp.broadcast_to(copy_choice, (rows, n)),
+    ]
+    used = iters * top + 1 + n
+    meta = jnp.concatenate(pieces + [jnp.zeros((rows, LANES - used), jnp.int32)], 1).astype(BF16)
+
+    me = lax.axis_index("expert")
+    state = tokens
+    meta_all = None
+    for step in range(iters):
+        state32 = state.astype(F32)
+        scale = lax.rsqrt(jnp.mean(state32 * state32, axis=1, keepdims=True) + 1e-06)
+        normed = (state32 * scale * norm_gain.astype(F32)).astype(BF16)
+        if step == 0:
+            both = gather(jnp.concatenate([normed, meta], 1))
+            x_all, meta_all = both[:, :width], both[:, width:]
+        else:
+            x_all = gather(normed)
+        own, other = run_ffn(step, x_all, meta_all, router, w_gate, w_up, w_down)
+        state = (state32 + scatter(own, other)).astype(BF16)
+
+    info = meta_all.astype(jnp.int32)
+    depth_all = info[:, iters * top]
+    copies = info[:, iters * top + 1:iters * top + 1 + n]
+    ids = jnp.arange(n, dtype=jnp.int32)
+    second = replica_plan[me]
+    home_copy = jnp.sum(jnp.where(ids == me, copies, 0), axis=1)
+    home_plan = jnp.sum(jnp.where(home_copy[:, None] == ids, replica_plan, 0), axis=1)
+    home_away = (home_plan == me) & (home_copy != me)
+    here = jnp.sum(jnp.where(ids == second, copies, 0), axis=1) == me
+    loads = []
+    for t in range(iters):
+        live = depth_all > t
+        picks = info[:, t * top:(t + 1) * top]
+        names_me = jnp.any(picks == me, axis=1)
+        names_second = jnp.any(picks == second, axis=1) & (second != me)
+        loads.append(jnp.sum((live & names_me & ~home_away).astype(F32)))
+        loads.append(jnp.sum((live & names_second & here).astype(F32)))
+    copy_load = jnp.stack(loads)[None, :] / float(rows * top)
+    return (state, copy_load)
+
+
+def body(tokens, depths, routes, *rest):
+    n = lax.axis_size("expert")
+    rows = tokens.shape[0]
+    iters, _, top = routes.shape
+    dense = 2 * rows * top // n >= rows and iters * top + 1 + n <= LANES and n % 4 == 0
+    return (dense_body if dense else sparse_body)(tokens, depths, routes, *rest)
 
 
 def solution(mesh):

time: 191 us -> 110 us (0.58)
  blocking collectives: 107 us -> 0 us
  matrix products: 22.1 us -> 0 us
  waiting for transfers between devices: 21.2 us -> 43.2 us
  Pallas kernels: 0 us -> 20.2 us
  local copies, waits for them, and re-layouts: 20.2 us -> 4.42 us
  starting transfers between devices: 10.2 us -> 25.8 us
  other arithmetic: 8.94 us -> 14.6 us
    all_to_all x2 -> x0, blocking collectives: 63.6 us -> none  [body(): lax.all_to_all(outbound, 'expert', split_axis=0, concat_axis=0, tiled=True)]
    ppermute x0 -> x20, waiting for transfers between devices: none -> 43.2 us  [swap(): return lax.ppermute(x, 'expert', [(i, i ^ offset) for i in range(n)])]
    unnamed x1 -> x0, blocking collectives: 43 us -> none
    ppermute x0 -> x20, starting transfers between devices: none -> 25.8 us  [swap(): return lax.ppermute(x, 'expert', [(i, i ^ offset) for i in range(n)])]
    dot_general x8 -> x0, matrix products: 22.1 us -> none  [the longest x2 11.1 us: expert_ffn(): jnp.dot(hidden, down_w, preferred_element_type=jnp.float32)]
    all_to_all x2 -> x0, waiting for transfers between devices: 21.2 us -> none  [body(): lax.all_to_all(result, 'expert', split_axis=0, concat_axis=0, tiled=True)]
    pallas_call x0 -> x2, Pallas kernels: none -> 20.2 us  [run_ffn(): pl.pallas_call(functools.partial(ffn_kernel, step), out_shape=(half, half...]
    all_to_all x2 -> x0, starting transfers between devices: 10.2 us -> none  [body(): lax.all_to_all(result, 'expert', split_axis=0, concat_axis=0, tiled=True)]
  transfers between devices with their start and end apart: 2 -> 20, of which waited for: 1 -> 15; matrix products, arithmetic and copies ran while one was open for 3% -> 7% of each run, Pallas kernels for 0% -> 0%
where the time goes in v1:
time: 110 us
  waiting for transfers between devices  43.2 us (39%)
  starting transfers between devices  25.8 us (23%)
  Pallas kernels  20.2 us (18%)
  other arithmetic  14.6 us (13%)
  local copies, waits for them, and re-layouts  4.42 us (4%)
  between operations  1.53 us (1%)
    ppermute x20, waiting for transfers between devices, swap(): return lax.ppermute(x, 'expert', [(i, i ^ offset) for i in range(n)])  43.2 us
    ppermute x20, starting transfers between devices, swap(): return lax.ppermute(x, 'expert', [(i, i ^ offset) for i in range(n)])  25.8 us
    pallas_call x2, Pallas kernels, run_ffn(): pl.pallas_call(functools.partial(ffn_kernel, step), out_shape=(half, half...  20.2 us
    div x1, other arithmetic, dense_body(): copy_load = jnp.stack(loads)[None, :] / float(rows * top)  3.02 us
    add x2, other arithmetic, scatter(): plane = own.astype(F32) + swap(other, 1).astype(F32)  2.33 us
  transfers between devices with their start and end apart: 20, of which 15 were waited for; matrix products, arithmetic and copies ran while one was open for 7% of the time, Pallas kernels for 0%

profile of v1, /device:TPU:0, one launch (start us, length us, event | category | flops | bytes accessed | tf_op | source)
XLA Modules:
  0.0 109.7 jit_solution(15055186069830368902)
XLA Ops:
  5.6 3.1 %collective-permute-start = (bf16[16,2176]{1,0:T(8,128)(2,1)S(1)}, bf16[16,2176]{1,0:T(8,128)(2,1)S(1)}, u32[]{:S(2)}, u32[]{:S(2)}) collective-permute-start(bf16[16,2176]{1,0:T(8,128)(2,1)S(1)} %concatenate.35), channel_id=1, source_target_pairs={{0,4},{1,5},{2,6},{3,7},{4,0},{5,1},{6,2},{7,3},{8,12},{9,13},{10,... | collective-permute-start | bytes 208904 | tf_op jit(solution)/shard_map/ppermute | solution.py:165
  8.8 2.6 %collective-permute-start.1 = (bf16[16,2176]{1,0:T(8,128)(2,1)S(1)}, bf16[16,2176]{1,0:T(8,128)(2,1)S(1)}, u32[]{:S(2)}, u32[]{:S(2)}) collective-permute-start(bf16[16,2176]{1,0:T(8,128)(2,1)S(1)} %concatenate.35), channel_id=1, source_target_pairs={{0,8},{1,9},{2,10},{3,11},{4,12},{5,13},{6,14},{7,15},{8,0},{9,1},... | collective-permute-start | bytes 208904 | tf_op jit(solution)/shard_map/ppermute | solution.py:165
  11.4 4.9 %collective-permute-done.1 = bf16[16,2176]{1,0:T(8,128)(2,1)S(1)} collective-permute-done((bf16[16,2176]{1,0:T(8,128)(2,1)S(1)}, bf16[16,2176]{1,0:T(8,128)(2,1)S(1)}, u32[]{:S(2)}, u32[]{:S(2)}) %collective-permute-start.1) | collective-permute-done | bytes 69664 | tf_op jit(solution)/shard_map/ppermute | solution.py:165
  17.6 1.6 %collective-permute-start.3 = (bf16[64,2176]{1,0:T(8,128)(2,1)S(1)}, bf16[64,2176]{1,0:T(8,128)(2,1)S(1)}, u32[]{:S(2)}, u32[]{:S(2)}) collective-permute-start(bf16[64,2176]{1,0:T(8,128)(2,1)S(1)} %pad_maximum_fusion), channel_id=1, source_target_pairs={{0,2},{1,3},{2,0},{3,1},{4,6},{5,7},{6,4},{7,5},{8,10},{9,11},{10,... | collective-permute-start | bytes 835592 | tf_op jit(solution)/shard_map/ppermute | solution.py:165
  19.2 5.0 %collective-permute-done.3 = bf16[64,2176]{1,0:T(8,128)(2,1)S(1)} collective-permute-done((bf16[64,2176]{1,0:T(8,128)(2,1)S(1)}, bf16[64,2176]{1,0:T(8,128)(2,1)S(1)}, u32[]{:S(2)}, u32[]{:S(2)}) %collective-permute-start.3) | collective-permute-done | bytes 278560 | tf_op jit(solution)/shard_map/ppermute | solution.py:165
  28.1 10.1 %ffn0.1 = (bf16[128,2048]{1,0:T(8,128)(2,1)}, bf16[128,2048]{1,0:T(8,128)(2,1)}) custom-call(bf16[256,2048]{1,0:T(8,128)(2,1)} %slice.92.x_ref, bf16[256,128]{1,0:T(8,128)(2,1)} %get-tuple-element.31.meta_ref, bf16[2048,16]{1,0:T(8,128)(2,1)} %copy.20.router_ref, bf16[1,2048,768]{2,1,0:T(8,128)(2,1)} %gate_ref.3, bf16[1,2048,768]{2,1,0:T(8,128)(2,1)} %up_ref.3, ...), custom_call_target="tpu_custom_call" | custom-call | flops 2415919104 | bytes 9437184 | tf_op jit(solution)/shard_map/ffn0/pallas_call | solution.py:138
  38.4 2.0 %collective-permute-done.5 = bf16[128,2048]{1,0:T(8,128)(2,1)S(1)} collective-permute-done((bf16[128,2048]{1,0:T(8,128)(2,1)}, bf16[128,2048]{1,0:T(8,128)(2,1)S(1)}, u32[]{:S(2)}, u32[]{:S(2)}) %collective-permute-start.5) | collective-permute-done | bytes 524320 | tf_op jit(solution)/shard_map/ppermute | solution.py:165
  41.6 1.6 %collective-permute-start.6 = (bf16[64,2048]{1,0:T(8,128)(2,1)S(1)}, bf16[64,2048]{1,0:T(8,128)(2,1)S(1)}, u32[]{:S(2)}, u32[]{:S(2)}) collective-permute-start(bf16[64,2048]{1,0:T(8,128)(2,1)S(1)} %slice.140), channel_id=1, source_target_pairs={{0,2},{1,3},{2,0},{3,1},{4,6},{5,7},{6,4},{7,5},{8,10},{9,11},{10,... | collective-permute-start | bytes 786440 | tf_op jit(solution)/shard_map/ppermute | solution.py:165
  43.1 6.8 %collective-permute-done.6 = bf16[64,2048]{1,0:T(8,128)(2,1)S(1)} collective-permute-done((bf16[64,2048]{1,0:T(8,128)(2,1)S(1)}, bf16[64,2048]{1,0:T(8,128)(2,1)S(1)}, u32[]{:S(2)}, u32[]{:S(2)}) %collective-permute-start.6) | collective-permute-done | bytes 262176 | tf_op jit(solution)/shard_map/ppermute | solution.py:165
  50.1 2.0 %collective-permute-start.9 = (bf16[16,2048]{1,0:T(8,128)(2,1)S(1)}, bf16[16,2048]{1,0:T(8,128)(2,1)S(1)}, u32[]{:S(2)}, u32[]{:S(2)}) collective-permute-start(bf16[16,2048]{1,0:T(8,128)(2,1)S(1)} %get-tuple-element.40), channel_id=1, source_target_pairs={{0,12},{1,13},{2,14},{3,15},{4,8},{5,9},{6,10},{7,11},{8,4},{9,5},... | collective-permute-start | bytes 196616 | tf_op jit(solution)/shard_map/ppermute | solution.py:165
  52.7 1.8 %collective-permute-start.7 = (bf16[16,2048]{1,0:T(8,128)(2,1)S(1)}, bf16[16,2048]{1,0:T(8,128)(2,1)S(1)}, u32[]{:S(2)}, u32[]{:S(2)}) collective-permute-start(bf16[16,2048]{1,0:T(8,128)(2,1)S(1)} %get-tuple-element.39), channel_id=1, source_target_pairs={{0,4},{1,5},{2,6},{3,7},{4,0},{5,1},{6,2},{7,3},{8,12},{9,13},{10,... | collective-permute-start | bytes 196616 | tf_op jit(solution)/shard_map/ppermute | solution.py:165
  54.5 2.4 %collective-permute-done.9 = bf16[16,2048]{1,0:T(8,128)(2,1)S(1)} collective-permute-done((bf16[16,2048]{1,0:T(8,128)(2,1)S(1)}, bf16[16,2048]{1,0:T(8,128)(2,1)S(1)}, u32[]{:S(2)}, u32[]{:S(2)}) %collective-permute-start.9) | collective-permute-done | bytes 65568 | tf_op jit(solution)/shard_map/ppermute | solution.py:165
  57.0 1.8 %collective-permute-done.8 = bf16[16,2048]{1,0:T(8,128)(2,1)S(1)} collective-permute-done((bf16[16,2048]{1,0:T(8,128)(2,1)S(1)}, bf16[16,2048]{1,0:T(8,128)(2,1)S(1)}, u32[]{:S(2)}, u32[]{:S(2)}) %collective-permute-start.8) | collective-permute-done | bytes 65568 | tf_op jit(solution)/shard_map/ppermute | solution.py:165
  59.1 2.8 %collective-permute-start.11 = (bf16[16,2048]{1,0:T(8,128)(2,1)S(1)}, bf16[16,2048]{1,0:T(8,128)(2,1)S(1)}, u32[]{:S(2)}, u32[]{:S(2)}) collective-permute-start(bf16[16,2048]{1,0:T(8,128)(2,1)S(1)} %get-tuple-element.25), channel_id=1, source_target_pairs={{0,8},{1,9},{2,10},{3,11},{4,12},{5,13},{6,14},{7,15},{8,0},{9,1},... | collective-permute-start | bytes 196616 | tf_op jit(solution)/shard_map/ppermute | solution.py:165
  63.6 3.2 %collective-permute-done.11 = bf16[16,2048]{1,0:T(8,128)(2,1)S(1)} collective-permute-done((bf16[16,2048]{1,0:T(8,128)(2,1)S(1)}, bf16[16,2048]{1,0:T(8,128)(2,1)S(1)}, u32[]{:S(2)}, u32[]{:S(2)}) %collective-permute-start.11) | collective-permute-done | bytes 65568 | tf_op jit(solution)/shard_map/ppermute | solution.py:165
  68.2 1.6 %collective-permute-start.13 = (bf16[64,2048]{1,0:T(8,128)(2,1)S(1)}, bf16[64,2048]{1,0:T(8,128)(2,1)S(1)}, u32[]{:S(2)}, u32[]{:S(2)}) collective-permute-start(bf16[64,2048]{1,0:T(8,128)(2,1)S(1)} %pad_maximum_fusion.1), channel_id=1, source_target_pairs={{0,2},{1,3},{2,0},{3,1},{4,6},{5,7},{6,4},{7,5},{8,10},{9,11},{10,... | collective-permute-start | bytes 786440 | tf_op jit(solution)/shard_map/ppermute | solution.py:165
  69.8 4.8 %collective-permute-done.13 = bf16[64,2048]{1,0:T(8,128)(2,1)S(1)} collective-permute-done((bf16[64,2048]{1,0:T(8,128)(2,1)S(1)}, bf16[64,2048]{1,0:T(8,128)(2,1)S(1)}, u32[]{:S(2)}, u32[]{:S(2)}) %collective-permute-start.13) | collective-permute-done | bytes 262176 | tf_op jit(solution)/shard_map/ppermute | solution.py:165
  74.8 1.9 %collective-permute-done.14 = bf16[128,2048]{1,0:T(8,128)(2,1)S(1)} collective-permute-done((bf16[128,2048]{1,0:T(8,128)(2,1)S(1)}, bf16[128,2048]{1,0:T(8,128)(2,1)S(1)}, u32[]{:S(2)}, u32[]{:S(2)}) %collective-permute-start.14) | collective-permute-done | bytes 524320 | tf_op jit(solution)/shard_map/ppermute | solution.py:165
  77.7 10.1 %ffn1.1 = (bf16[128,2048]{1,0:T(8,128)(2,1)}, bf16[128,2048]{1,0:T(8,128)(2,1)}) custom-call(bf16[256,2048]{1,0:T(8,128)(2,1)} %copy-done, bf16[256,128]{1,0:T(8,128)(2,1)} %get-tuple-element.31.meta_ref, bf16[2048,16]{1,0:T(8,128)(2,1)} %copy.20.router_ref, bf16[1,2048,768]{2,1,0:T(8,128)(2,1)} %gate_ref.3, bf16[1,2048,768]{2,1,0:T(8,128)(2,1)} %up_ref.3, ...), custom_call_target="tpu_custom_call" | custom-call | flops 2415919104 | bytes 9437184 | tf_op jit(solution)/shard_map/ffn1/pallas_call | solution.py:138
  91.5 1.6 %collective-permute-start.16 = (bf16[64,2048]{1,0:T(8,128)(2,1)S(1)}, bf16[64,2048]{1,0:T(8,128)(2,1)S(1)}, u32[]{:S(2)}, u32[]{:S(2)}) collective-permute-start(bf16[64,2048]{1,0:T(8,128)(2,1)S(1)} %slice.139), channel_id=1, source_target_pairs={{0,2},{1,3},{2,0},{3,1},{4,6},{5,7},{6,4},{7,5},{8,10},{9,11},{10,... | collective-permute-start | bytes 786440 | tf_op jit(solution)/shard_map/ppermute | solution.py:165
  94.8 5.3 %collective-permute-done.16 = bf16[64,2048]{1,0:T(8,128)(2,1)S(1)} collective-permute-done((bf16[64,2048]{1,0:T(8,128)(2,1)S(1)}, bf16[64,2048]{1,0:T(8,128)(2,1)S(1)}, u32[]{:S(2)}, u32[]{:S(2)}) %collective-permute-start.16) | collective-permute-done | bytes 262176 | tf_op jit(solution)/shard_map/ppermute | solution.py:165
  100.2 1.6 %collective-permute-start.19 = (bf16[16,2048]{1,0:T(8,128)(2,1)S(1)}, bf16[16,2048]{1,0:T(8,128)(2,1)S(1)}, u32[]{:S(2)}, u32[]{:S(2)}) collective-permute-start(bf16[16,2048]{1,0:T(8,128)(2,1)S(1)} %get-tuple-element.35), channel_id=1, source_target_pairs={{0,12},{1,13},{2,14},{3,15},{4,8},{5,9},{6,10},{7,11},{8,4},{9,5},... | collective-permute-start | bytes 196616 | tf_op jit(solution)/shard_map/ppermute | solution.py:165
  102.6 2.1 %collective-permute-start.17 = (bf16[16,2048]{1,0:T(8,128)(2,1)S(1)}, bf16[16,2048]{1,0:T(8,128)(2,1)S(1)}, u32[]{:S(2)}, u32[]{:S(2)}) collective-permute-start(bf16[16,2048]{1,0:T(8,128)(2,1)S(1)} %get-tuple-element.34), channel_id=1, source_target_pairs={{0,4},{1,5},{2,6},{3,7},{4,0},{5,1},{6,2},{7,3},{8,12},{9,13},{10,... | collective-permute-start | bytes 196616 | tf_op jit(solution)/shard_map/ppermute | solution.py:165
  104.7 3.0 %maximum_multiply_fusion = f32[1,4]{1,0:T(1,128)} fusion(f32[1,1]{1,0:T(1,128)} %bitcast.8, f32[1,1]{1,0:T(1,128)} %bitcast.7, f32[1,1]{1,0:T(1,128)} %bitcast.6, f32[1,1]{1,0:T(1,128)} %bitcast.4), kind=kLoop, calls=%fused_computation.71 | loop fusion | flops 16 | bytes 32 | tf_op jit(solution)/shard_map/div | solution.py:223
  (77 shorter events, 24.4 us)
Async XLA Ops:
  5.6 18.7 %copy-start.2 = (bf16[2048,16]{0,1:T(8,128)(2,1)S(1)}, bf16[2048,16]{0,1:T(8,128)(2,1)}, u32[]{:S(2)}) copy-start(bf16[2048,16]{0,1:T(8,128)(2,1)} %param.14) | copy-start | bytes 196612
  5.6 5.7 %collective-permute-start = (bf16[16,2176]{1,0:T(8,128)(2,1)S(1)}, bf16[16,2176]{1,0:T(8,128)(2,1)S(1)}, u32[]{:S(2)}, u32[]{:S(2)}) collective-permute-start(bf16[16,2176]{1,0:T(8,128)(2,1)S(1)} %concatenate.35), channel_id=1, source_target_pairs={{0,4},{1,5},{2,6},{3,7},{4,0},{5,1},{6,2},{7,3},{8,12},{9,13},{10,... | collective-permute-start | bytes 208904 | tf_op jit(solution)/shard_map/ppermute | solution.py:165
  8.8 7.5 %collective-permute-start.1 = (bf16[16,2176]{1,0:T(8,128)(2,1)S(1)}, bf16[16,2176]{1,0:T(8,128)(2,1)S(1)}, u32[]{:S(2)}, u32[]{:S(2)}) collective-permute-start(bf16[16,2176]{1,0:T(8,128)(2,1)S(1)} %concatenate.35), channel_id=1, source_target_pairs={{0,8},{1,9},{2,10},{3,11},{4,12},{5,13},{6,14},{7,15},{8,0},{9,1},... | collective-permute-start | bytes 208904 | tf_op jit(solution)/shard_map/ppermute | solution.py:165
  11.3 6.2 %collective-permute-start.2 = (bf16[16,2176]{1,0:T(8,128)(2,1)S(1)}, bf16[16,2176]{1,0:T(8,128)(2,1)S(1)}, u32[]{:S(2)}, u32[]{:S(2)}) collective-permute-start(bf16[16,2176]{1,0:T(8,128)(2,1)S(1)} %concatenate.35), channel_id=1, source_target_pairs={{0,12},{1,13},{2,14},{3,15},{4,8},{5,9},{6,10},{7,11},{8,4},{9,5},... | collective-permute-start | bytes 208904 | tf_op jit(solution)/shard_map/ppermute | solution.py:165
  17.6 6.7 %collective-permute-start.3 = (bf16[64,2176]{1,0:T(8,128)(2,1)S(1)}, bf16[64,2176]{1,0:T(8,128)(2,1)S(1)}, u32[]{:S(2)}, u32[]{:S(2)}) collective-permute-start(bf16[64,2176]{1,0:T(8,128)(2,1)S(1)} %pad_maximum_fusion), channel_id=1, source_target_pairs={{0,2},{1,3},{2,0},{3,1},{4,6},{5,7},{6,4},{7,5},{8,10},{9,11},{10,... | collective-permute-start | bytes 835592 | tf_op jit(solution)/shard_map/ppermute | solution.py:165
  24.3 2.0 %collective-permute-start.4 = (bf16[128,2176]{1,0:T(8,128)(2,1)S(1)}, bf16[128,2176]{1,0:T(8,128)(2,1)S(1)}, u32[]{:S(2)}, u32[]{:S(2)}) collective-permute-start(bf16[128,2176]{1,0:T(8,128)(2,1)S(1)} %get-tuple-element.32), channel_id=1, source_target_pairs={{0,1},{1,0},{2,3},{3,2},{4,5},{5,4},{6,7},{7,6},{8,9},{9,8},{10,11... | collective-permute-start | bytes 1671176 | tf_op jit(solution)/shard_map/ppermute | solution.py:165
  38.2 2.1 %collective-permute-start.5 = (bf16[128,2048]{1,0:T(8,128)(2,1)}, bf16[128,2048]{1,0:T(8,128)(2,1)S(1)}, u32[]{:S(2)}, u32[]{:S(2)}) collective-permute-start(bf16[128,2048]{1,0:T(8,128)(2,1)} %get-tuple-element.7), channel_id=1, source_target_pairs={{0,1},{1,0},{2,3},{3,2},{4,5},{5,4},{6,7},{7,6},{8,9},{9,8},{10,11... | collective-permute-start | bytes 1572872 | tf_op jit(solution)/shard_map/ppermute | solution.py:165
  41.6 17.2 %copy-start.1 = (bf16[16,2048]{1,0:T(8,128)(2,1)S(1)}, bf16[16,2048]{1,0:T(8,128)(2,1)}, u32[]{:S(2)}) copy-start(bf16[16,2048]{1,0:T(8,128)(2,1)} %param.10) | copy-start | bytes 196612
  41.6 8.4 %collective-permute-start.6 = (bf16[64,2048]{1,0:T(8,128)(2,1)S(1)}, bf16[64,2048]{1,0:T(8,128)(2,1)S(1)}, u32[]{:S(2)}, u32[]{:S(2)}) collective-permute-start(bf16[64,2048]{1,0:T(8,128)(2,1)S(1)} %slice.140), channel_id=1, source_target_pairs={{0,2},{1,3},{2,0},{3,1},{4,6},{5,7},{6,4},{7,5},{8,10},{9,11},{10,... | collective-permute-start | bytes 786440 | tf_op jit(solution)/shard_map/ppermute | solution.py:165
  50.1 6.9 %collective-permute-start.9 = (bf16[16,2048]{1,0:T(8,128)(2,1)S(1)}, bf16[16,2048]{1,0:T(8,128)(2,1)S(1)}, u32[]{:S(2)}, u32[]{:S(2)}) collective-permute-start(bf16[16,2048]{1,0:T(8,128)(2,1)S(1)} %get-tuple-element.40), channel_id=1, source_target_pairs={{0,12},{1,13},{2,14},{3,15},{4,8},{5,9},{6,10},{7,11},{8,4},{9,5},... | collective-permute-start | bytes 196616 | tf_op jit(solution)/shard_map/ppermute | solution.py:165
  52.1 6.7 %collective-permute-start.8 = (bf16[16,2048]{1,0:T(8,128)(2,1)S(1)}, bf16[16,2048]{1,0:T(8,128)(2,1)S(1)}, u32[]{:S(2)}, u32[]{:S(2)}) collective-permute-start(bf16[16,2048]{1,0:T(8,128)(2,1)S(1)} %get-tuple-element.41), channel_id=1, source_target_pairs={{0,8},{1,9},{2,10},{3,11},{4,12},{5,13},{6,14},{7,15},{8,0},{9,1},... | collective-permute-start | bytes 196616 | tf_op jit(solution)/shard_map/ppermute | solution.py:165
  52.7 6.0 %collective-permute-start.7 = (bf16[16,2048]{1,0:T(8,128)(2,1)S(1)}, bf16[16,2048]{1,0:T(8,128)(2,1)S(1)}, u32[]{:S(2)}, u32[]{:S(2)}) collective-permute-start(bf16[16,2048]{1,0:T(8,128)(2,1)S(1)} %get-tuple-element.39), channel_id=1, source_target_pairs={{0,4},{1,5},{2,6},{3,7},{4,0},{5,1},{6,2},{7,3},{8,12},{9,13},{10,... | collective-permute-start | bytes 196616 | tf_op jit(solution)/shard_map/ppermute | solution.py:165
  59.0 4.6 %collective-permute-start.10 = (bf16[16,2048]{1,0:T(8,128)(2,1)S(1)}, bf16[16,2048]{1,0:T(8,128)(2,1)S(1)}, u32[]{:S(2)}, u32[]{:S(2)}) collective-permute-start(bf16[16,2048]{1,0:T(8,128)(2,1)S(1)} %get-tuple-element.25), channel_id=1, source_target_pairs={{0,4},{1,5},{2,6},{3,7},{4,0},{5,1},{6,2},{7,3},{8,12},{9,13},{10,... | collective-permute-start | bytes 196616 | tf_op jit(solution)/shard_map/ppermute | solution.py:165
  59.1 7.7 %collective-permute-start.11 = (bf16[16,2048]{1,0:T(8,128)(2,1)S(1)}, bf16[16,2048]{1,0:T(8,128)(2,1)S(1)}, u32[]{:S(2)}, u32[]{:S(2)}) collective-permute-start(bf16[16,2048]{1,0:T(8,128)(2,1)S(1)} %get-tuple-element.25), channel_id=1, source_target_pairs={{0,8},{1,9},{2,10},{3,11},{4,12},{5,13},{6,14},{7,15},{8,0},{9,1},... | collective-permute-start | bytes 196616 | tf_op jit(solution)/shard_map/ppermute | solution.py:165
  62.0 6.2 %collective-permute-start.12 = (bf16[16,2048]{1,0:T(8,128)(2,1)S(1)}, bf16[16,2048]{1,0:T(8,128)(2,1)S(1)}, u32[]{:S(2)}, u32[]{:S(2)}) collective-permute-start(bf16[16,2048]{1,0:T(8,128)(2,1)S(1)} %get-tuple-element.25), channel_id=1, source_target_pairs={{0,12},{1,13},{2,14},{3,15},{4,8},{5,9},{6,10},{7,11},{8,4},{9,5},... | collective-permute-start | bytes 196616 | tf_op jit(solution)/shard_map/ppermute | solution.py:165
  68.2 6.5 %collective-permute-start.13 = (bf16[64,2048]{1,0:T(8,128)(2,1)S(1)}, bf16[64,2048]{1,0:T(8,128)(2,1)S(1)}, u32[]{:S(2)}, u32[]{:S(2)}) collective-permute-start(bf16[64,2048]{1,0:T(8,128)(2,1)S(1)} %pad_maximum_fusion.1), channel_id=1, source_target_pairs={{0,2},{1,3},{2,0},{3,1},{4,6},{5,7},{6,4},{7,5},{8,10},{9,11},{10,... | collective-permute-start | bytes 786440 | tf_op jit(solution)/shard_map/ppermute | solution.py:165
  74.7 2.0 %collective-permute-start.14 = (bf16[128,2048]{1,0:T(8,128)(2,1)S(1)}, bf16[128,2048]{1,0:T(8,128)(2,1)S(1)}, u32[]{:S(2)}, u32[]{:S(2)}) collective-permute-start(bf16[128,2048]{1,0:T(8,128)(2,1)S(1)} %get-tuple-element.37), channel_id=1, source_target_pairs={{0,1},{1,0},{2,3},{3,2},{4,5},{5,4},{6,7},{7,6},{8,9},{9,8},{10,11... | collective-permute-start | bytes 1572872 | tf_op jit(solution)/shard_map/ppermute | solution.py:165
  76.7 1.0 copy-start
  77.7 10.3 %copy-start.3 = (s32[16]{0:T(128)S(1)}, s32[16]{0:T(128)}, u32[]{:S(2)}) copy-start(s32[16]{0:T(128)} %param.18) | copy-start | bytes 196
  87.8 2.5 %collective-permute-start.15 = (bf16[128,2048]{1,0:T(8,128)(2,1)}, bf16[128,2048]{1,0:T(8,128)(2,1)S(1)}, u32[]{:S(2)}, u32[]{:S(2)}) collective-permute-start(bf16[128,2048]{1,0:T(8,128)(2,1)} %get-tuple-element.9), channel_id=1, source_target_pairs={{0,1},{1,0},{2,3},{3,2},{4,5},{5,4},{6,7},{7,6},{8,9},{9,8},{10,11... | collective-permute-start | bytes 1572872 | tf_op jit(solution)/shard_map/ppermute | solution.py:165
  91.5 8.6 %collective-permute-start.16 = (bf16[64,2048]{1,0:T(8,128)(2,1)S(1)}, bf16[64,2048]{1,0:T(8,128)(2,1)S(1)}, u32[]{:S(2)}, u32[]{:S(2)}) collective-permute-start(bf16[64,2048]{1,0:T(8,128)(2,1)S(1)} %slice.139), channel_id=1, source_target_pairs={{0,2},{1,3},{2,0},{3,1},{4,6},{5,7},{6,4},{7,5},{8,10},{9,11},{10,... | collective-permute-start | bytes 786440 | tf_op jit(solution)/shard_map/ppermute | solution.py:165
  100.2 7.5 %collective-permute-start.19 = (bf16[16,2048]{1,0:T(8,128)(2,1)S(1)}, bf16[16,2048]{1,0:T(8,128)(2,1)S(1)}, u32[]{:S(2)}, u32[]{:S(2)}) collective-permute-start(bf16[16,2048]{1,0:T(8,128)(2,1)S(1)} %get-tuple-element.35), channel_id=1, source_target_pairs={{0,12},{1,13},{2,14},{3,15},{4,8},{5,9},{6,10},{7,11},{8,4},{9,5},... | collective-permute-start | bytes 196616 | tf_op jit(solution)/shard_map/ppermute | solution.py:165
  101.8 7.2 %collective-permute-start.18 = (bf16[16,2048]{1,0:T(8,128)(2,1)S(1)}, bf16[16,2048]{1,0:T(8,128)(2,1)S(1)}, u32[]{:S(2)}, u32[]{:S(2)}) collective-permute-start(bf16[16,2048]{1,0:T(8,128)(2,1)S(1)} %get-tuple-element.36), channel_id=1, source_target_pairs={{0,8},{1,9},{2,10},{3,11},{4,12},{5,13},{6,14},{7,15},{8,0},{9,1},... | collective-permute-start | bytes 196616 | tf_op jit(solution)/shard_map/ppermute | solution.py:165
  102.6 6.5 %collective-permute-start.17 = (bf16[16,2048]{1,0:T(8,128)(2,1)S(1)}, bf16[16,2048]{1,0:T(8,128)(2,1)S(1)}, u32[]{:S(2)}, u32[]{:S(2)}) collective-permute-start(bf16[16,2048]{1,0:T(8,128)(2,1)S(1)} %get-tuple-element.34), channel_id=1, source_target_pairs={{0,4},{1,5},{2,6},{3,7},{4,0},{5,1},{6,2},{7,3},{8,12},{9,13},{10,... | collective-permute-start | bytes 196616 | tf_op jit(solution)/shard_map/ppermute | solution.py:165

commit v2 on v1

--- a/solution.py
+++ b/solution.py
@@ -88,61 +88,194 @@
     return (state, copy_load)
 
 
-def ffn_kernel(step, x_ref, meta_ref, router_ref, gate_ref, up_ref, down_ref, own_ref, other_ref,
-               hidden_ref):
-    rows, width = x_ref.shape
-    top = 8
-    ff = gate_ref.shape[-1]
-    experts = router_ref.shape[1]
+VMEM = pl.BlockSpec(memory_space=pltpu.VMEM)
+HBM = pl.BlockSpec(memory_space=pltpu.HBM)
+
+
+def dot_t(a, b):
+    return lax.dot_general(a, b, (((1,), (1,)), ((), ())), preferred_element_type=F32)
+
+
+def norm_rows(state32, gain):
+    mean = jnp.mean(state32 * state32, axis=1, keepdims=True)
+    return (state32 * lax.rsqrt(mean + 1e-06) * gain).astype(BF16)
+
+
+def open_kernel(*refs):
+    args, out_ref, held, sems = refs[:5], refs[5], refs[6:11], refs[11]
+    moves = [pltpu.make_async_copy(a, h, sems.at[i]) for i, (a, h) in enumerate(zip(args, held))]
+    for m in moves:
+        m.start()
+    for m in moves:
+        m.wait()
+    tokens_ref, gain_ref, routes_ref, depths_ref, copies_ref = held
+    rows, width = tokens_ref.shape
+    iters, top, _ = routes_ref.shape
+    n = copies_ref.shape[1]
+    out_ref[:, :width] = norm_rows(
+        tokens_ref[...].astype(F32), gain_ref[...].astype(F32).reshape(1, width)
+    )
+    expert = lax.broadcasted_iota(jnp.int32, (n, rows), 0)
+    parts = []
+    for t in range(iters):
+        live = depths_ref[...] > t
+        named = jnp.zeros((n, rows), F32)
+        for k in range(top):
+            named = jnp.where((routes_ref[t, k:k + 1, :] == expert) & live, 1.0, named)
+        parts.append(named)
+    square = (n, n)
+    diag = lax.broadcasted_iota(jnp.int32, square, 0) == lax.broadcasted_iota(jnp.int32, square, 1)
+    copies = jnp.where(diag, jnp.broadcast_to(copies_ref[...], square).astype(F32), 0.0)
+    parts.append(jnp.broadcast_to(jnp.sum(copies, axis=1, keepdims=True), (n, rows)))
+    parts.append(jnp.zeros((LANES - (iters + 1) * n, rows), F32))
+    table = jnp.concatenate(parts, 0).astype(BF16)
+    square = (rows, rows)
+    eye = lax.broadcasted_iota(jnp.int32, square, 0) == lax.broadcasted_iota(jnp.int32, square, 1)
+    meta = dot_t(jnp.where(eye, 1.0, 0.0).astype(BF16), table)
+    out_ref[:, width:] = meta.astype(BF16)
+
+
+def run_open(tokens, gain, routes, depths, copies):
+    rows, width = tokens.shape
+    args = tuple(pltpu.with_memory_space_constraint(x, pltpu.HBM) for x in (tokens, gain, routes, depths, copies))
+    return pl.pallas_call(
+        open_kernel,
+        out_shape=jax.ShapeDtypeStruct((rows, width + LANES), BF16),
+        in_specs=[HBM] * 5,
+        out_specs=VMEM,
+        scratch_shapes=[pltpu.VMEM(x.shape, x.dtype) for x in args]
+        + [pltpu.SemaphoreType.DMA((len(args),))],
+        compiler_params=pltpu.CompilerParams(vmem_limit_bytes=4 << 20),
+        name="open_rows",
+    )(*args)
+
+
+CHUNKS = 4
+
+
+def load_kernel(*refs):
+    count = len(refs) // 2
+    sems = refs[-1]
+    copies = []
+    for i in range(count):
+        src, dst = refs[i], refs[count + i]
+        size = src.shape[1] // CHUNKS
+        for j in range(CHUNKS):
+            part = pl.ds(j * size, size)
+            copies.append(
+                pltpu.make_async_copy(src.at[:, part], dst.at[:, part], sems.at[i, j])
+            )
+    for c in copies:
+        c.start()
+    for c in copies:
+        c.wait()
+
+
+def run_load(*weights):
+    size = sum(w.size for w in weights)
+    weights = tuple(pltpu.with_memory_space_constraint(w, pltpu.HBM) for w in weights)
+    return pl.pallas_call(
+        load_kernel,
+        out_shape=tuple(jax.ShapeDtypeStruct(w.shape, w.dtype) for w in weights),
+        in_specs=[HBM] * len(weights),
+        out_specs=(VMEM,) * len(weights),
+        scratch_shapes=[pltpu.SemaphoreType.DMA((len(weights), CHUNKS))],
+        compiler_params=pltpu.CompilerParams(vmem_limit_bytes=1 << 20),
+        cost_estimate=pl.CostEstimate(flops=0, bytes_accessed=4 * size, transcendentals=0),
+        name="load_weights",
+    )(*weights)
+
+
+def count_kernel(iters, scale, meta_ref, plan_ref, load_ref):
+    meta_col = meta_ref.shape[1] - LANES
+    n = plan_ref.shape[1]
+    me = lax.axis_index("expert").astype(F32)
+    meta = meta_ref[:, meta_col:].astype(F32)
+    rows = meta.shape[0]
+    lane = lax.broadcasted_iota(jnp.int32, (rows, LANES), 1).astype(F32)
+    ids = lax.broadcasted_iota(jnp.int32, (rows, n), 1).astype(F32)
+    plan = jnp.broadcast_to(plan_ref[...].astype(F32), (rows, n))
+
+    def at(index):
+        return jnp.sum(jnp.where(lane == index, meta, 0.0), axis=1, keepdims=True)
+
+    first = float(iters * n)
+    second = jnp.sum(jnp.where(ids == me, plan, 0.0), axis=1, keepdims=True)
+    home_copy = at(me + first)
+    home_plan = jnp.sum(jnp.where(ids == home_copy, plan, 0.0), axis=1, keepdims=True)
+    at_home = jnp.where((home_plan == me) & (home_copy != me), 0.0, 1.0)
+    at_copy = jnp.where((at(second + first) == me) & (second != me), 1.0, 0.0)
+    slot = lax.broadcasted_iota(jnp.int32, (1, 2 * iters), 1)
+    loads = jnp.zeros((1, 2 * iters), F32)
+    for t in range(iters):
+        for j, (which, served) in enumerate(((me, at_home), (second, at_copy))):
+            pairs = jnp.sum(at(which + float(t * n)) * served, axis=0, keepdims=True)
+            loads = jnp.where(slot == 2 * t + j, pairs, loads)
+    load_ref[...] = loads / scale
+
+
+def run_count(iters, scale, meta, plan):
+    return pl.pallas_call(
+        functools.partial(count_kernel, iters, scale),
+        out_shape=jax.ShapeDtypeStruct((1, 2 * iters), F32),
+        in_specs=[VMEM] * 2,
+        out_specs=VMEM,
+        compiler_params=pltpu.CompilerParams(vmem_limit_bytes=4 << 20),
+        cost_estimate=pl.CostEstimate(flops=0, bytes_accessed=1 << 20, transcendentals=0),
+        name="count_pairs",
+    )(meta, plan)
+
+
+def ffn_kernel(step, x_ref, meta_ref, router_ref, gate_ref, up_ref, down_ref,
+               own_ref, other_ref, hidden_ref):
+    rows = x_ref.shape[0]
+    width, ff = gate_ref.shape[1:]
+    n = router_ref.shape[0]
+    meta_col = meta_ref.shape[1] - LANES
     me = lax.axis_index("expert")
-    x = x_ref[...]
-    logits = jnp.dot(x, router_ref[...], preferred_element_type=F32)
-    sig = jax.nn.sigmoid(logits)
-    meta = meta_ref[...].astype(F32)
-    ids = lax.broadcasted_iota(jnp.int32, (rows, experts), 1)
-    idf = ids.astype(F32)
-    named = jnp.zeros((rows, experts), F32)
-    for k in range(top):
-        c = step * top + k
-        named = jnp.where(meta[:, c:c + 1] == idf, 1.0, named)
-    sig = jnp.where(named > 0.0, sig, 0.0)
+
+    routers = jnp.concatenate([router_ref[...]] * (LANES // n), 0)
+    logits = dot_t(x_ref[:, :width], routers)
+    lane = lax.broadcasted_iota(jnp.int32, (rows, LANES), 1)
+    named = (meta_ref[:, meta_col:].astype(F32) > 0.0) & (lane >= step * n) & (lane < (step + 1) * n)
+    sig = jnp.where(named, jax.nn.sigmoid(logits), 0.0)
     total = jnp.sum(sig, axis=1, keepdims=True)
-    mine = jnp.sum(jnp.where(ids == me, sig, 0.0), axis=1, keepdims=True)
-    depth = meta[:, 2 * top:2 * top + 1]
-    weight = jnp.where(depth > float(step), mine / total, 0.0)
-
-    tile = 256
-
-    @pl.loop(0, ff // tile)
-    def _(i):
-        cols = pl.ds(pl.multiple_of(i * tile, tile), tile)
-        g = jnp.dot(x_ref[...], gate_ref[0, :, cols], preferred_element_type=F32)
-        u = jnp.dot(x_ref[...], up_ref[0, :, cols], preferred_element_type=F32)
-        hidden_ref[:, cols] = (g * jax.nn.sigmoid(g) * u).astype(BF16)
+    at_me = lane == step * n + me
+    mine = jnp.sum(jnp.where(at_me, sig, 0.0), axis=1, keepdims=True)
+    here = jnp.sum(jnp.where(at_me & named, 1.0, 0.0), axis=1, keepdims=True)
+    weight = jnp.where(here > 0.0, mine / total, 0.0)
+
+    g = jnp.dot(x_ref[:, :width], gate_ref[0], preferred_element_type=F32)
+    u = jnp.dot(x_ref[:, :width], up_ref[0], preferred_element_type=F32)
+    hidden_ref[...] = (g * jax.nn.sigmoid(g) * u).astype(BF16)
 
     half = rows // 2
+    tile = 512
 
     @pl.loop(0, width // tile)
     def _(i):
         cols = pl.ds(pl.multiple_of(i * tile, tile), tile)
         o = jnp.dot(hidden_ref[...], down_ref[0, :, cols], preferred_element_type=F32)
         o = o.astype(BF16).astype(F32) * weight
-        own_ref[:, cols] = o[:half].astype(BF16)
+        own_ref[:, cols] = o[:half]
         other_ref[:, cols] = o[half:].astype(BF16)
 
 
 def run_ffn(step, x, meta, router, w_gate, w_up, w_down):
-    rows, width = x.shape
-    ff = w_gate.shape[-1]
-    half = jax.ShapeDtypeStruct((rows // 2, width), BF16)
+    rows = x.shape[0]
+    width, ff = w_gate.shape[1:]
     return pl.pallas_call(
         functools.partial(ffn_kernel, step),
-        out_shape=(half, half),
-        in_specs=[pl.BlockSpec(memory_space=pltpu.VMEM)] * 6,
-        out_specs=(pl.BlockSpec(memory_space=pltpu.VMEM),) * 2,
+        out_shape=(
+            jax.ShapeDtypeStruct((rows // 2, width), F32),
+            jax.ShapeDtypeStruct((rows // 2, width), BF16),
+        ),
+        in_specs=[VMEM] * 6,
+        out_specs=(VMEM,) * 2,
         scratch_shapes=[pltpu.VMEM((rows, ff), BF16)],
+        compiler_params=pltpu.CompilerParams(vmem_limit_bytes=16 << 20),
         cost_estimate=pl.CostEstimate(
-            flops=6 * rows * width * ff, bytes_accessed=6 * width * ff, transcendentals=rows * ff
+            flops=6 * rows * width * ff, bytes_accessed=4 * rows * width, transcendentals=rows * ff
         ),
         name=f"ffn{step}",
     )(x, meta, router, w_gate, w_up, w_down)
@@ -160,18 +293,20 @@
         ny *= 2
     nz = chips // ny
     zs = 2 * ny
+    gain = norm_gain[None, :]
 
     def swap(x, offset):
         return lax.ppermute(x, "expert", [(i, i ^ offset) for i in range(n)])
 
-    def gather(x):
+    def gather(x, beside=()):
         zb = [x] + [swap(x, a * zs) for a in range(1, nz)]
+        zb, beside = lax.optimization_barrier((zb, beside))
         z_all = jnp.concatenate(zb, 0)
         plane = jnp.concatenate([z_all] + [swap(z_all, b * 2) for b in range(1, ny)], 0)
-        return jnp.concatenate([plane, swap(plane, 1)], 0)
+        return jnp.concatenate([plane, swap(plane, 1)], 0), beside
 
     def scatter(own, other):
-        plane = own.astype(F32) + swap(other, 1).astype(F32)
+        plane = own + swap(other, 1).astype(F32)
         r = rows * nz
         acc = plane[:r]
         for b in range(1, ny):
@@ -181,46 +316,21 @@
             out = out + swap(acc[a * rows:(a + 1) * rows].astype(BF16), a * zs).astype(F32)
         return out
 
-    pieces = [routes[t] for t in range(iters)] + [
-        depths[:, None],
-        jnp.broadcast_to(copy_choice, (rows, n)),
-    ]
-    used = iters * top + 1 + n
-    meta = jnp.concatenate(pieces + [jnp.zeros((rows, LANES - used), jnp.int32)], 1).astype(BF16)
-
-    me = lax.axis_index("expert")
+    block = run_open(
+        tokens, norm_gain, jnp.transpose(routes, (0, 2, 1)), depths[None, :], copy_choice
+    )
+    block, w_gate, w_up, w_down = lax.optimization_barrier((block, w_gate, w_up, w_down))
+    weights = run_load(w_gate, w_up, w_down)
     state = tokens
-    meta_all = None
+    meta = None
     for step in range(iters):
-        state32 = state.astype(F32)
-        scale = lax.rsqrt(jnp.mean(state32 * state32, axis=1, keepdims=True) + 1e-06)
-        normed = (state32 * scale * norm_gain.astype(F32)).astype(BF16)
+        x_all, weights = gather(block, weights)
         if step == 0:
-            both = gather(jnp.concatenate([normed, meta], 1))
-            x_all, meta_all = both[:, :width], both[:, width:]
-        else:
-            x_all = gather(normed)
-        own, other = run_ffn(step, x_all, meta_all, router, w_gate, w_up, w_down)
-        state = (state32 + scatter(own, other)).astype(BF16)
-
-    info = meta_all.astype(jnp.int32)
-    depth_all = info[:, iters * top]
-    copies = info[:, iters * top + 1:iters * top + 1 + n]
-    ids = jnp.arange(n, dtype=jnp.int32)
-    second = replica_plan[me]
-    home_copy = jnp.sum(jnp.where(ids == me, copies, 0), axis=1)
-    home_plan = jnp.sum(jnp.where(home_copy[:, None] == ids, replica_plan, 0), axis=1)
-    home_away = (home_plan == me) & (home_copy != me)
-    here = jnp.sum(jnp.where(ids == second, copies, 0), axis=1) == me
-    loads = []
-    for t in range(iters):
-        live = depth_all > t
-        picks = info[:, t * top:(t + 1) * top]
-        names_me = jnp.any(picks == me, axis=1)
-        names_second = jnp.any(picks == second, axis=1) & (second != me)
-        loads.append(jnp.sum((live & names_me & ~home_away).astype(F32)))
-        loads.append(jnp.sum((live & names_second & here).astype(F32)))
-    copy_load = jnp.stack(loads)[None, :] / float(rows * top)
+            meta = x_all
+            copy_load = run_count(iters, float(rows * top), meta, replica_plan[None, :])
+        own, other = run_ffn(step, x_all, meta, router.T, *weights)
+        state = (state.astype(F32) + scatter(own, other)).astype(BF16)
+        block = norm_rows(state.astype(F32), gain.astype(F32))
     return (state, copy_load)
 
 
@@ -228,7 +338,7 @@
     n = lax.axis_size("expert")
     rows = tokens.shape[0]
     iters, _, top = routes.shape
-    dense = 2 * rows * top // n >= rows and iters * top + 1 + n <= LANES and n % 4 == 0
+    dense = 2 * rows * top // n >= rows and (iters + 1) * n <= LANES and LANES % n == 0 and n % 4 == 0
     return (dense_body if dense else sparse_body)(tokens, depths, routes, *rest)
 
 

time: 110 us -> 86.4 us (0.79)
  other arithmetic: 14.6 us -> 1.33 us
  Pallas kernels: 20.2 us -> 12.9 us
  local copies, waits for them, and re-layouts: 4.42 us -> 0.4 us
  waiting for transfers between devices: 43.2 us -> 44.8 us
    pallas_call x2 -> x5, Pallas kernels: 20.2 us -> 12.9 us  [the longest x2 7.16 us: run_ffn(): pl.pallas_call(functools.partial(ffn_kernel, step), out_shape=(jax.ShapeD...]
    div x1 -> x0, other arithmetic: 3.02 us -> none  [dense_body(): copy_load = jnp.stack(loads)[None, :] / float(rows * top)]
    convert_element_type x4 -> x3, other arithmetic: 2.92 us -> 0.77 us  [the longest x1 0.67 us: dense_body(): state = (state.astype(F32) + scatter(own, other)).astype(BF16)]
    add x2, other arithmetic: 2.33 us -> 0.22 us  [scatter(): plane = own + swap(other, 1).astype(F32)]
    reduce_sum x5 -> x1, other arithmetic: 2.18 us -> 0.16 us  [norm_rows(): mean = jnp.mean(state32 * state32, axis=1, keepdims=True)]
    unnamed x17 -> x16, local copies, waits for them, and re-layouts: 2.09 us -> 0.13 us
    ppermute x20, waiting for transfers between devices: 43.2 us -> 44.8 us  [swap(): return lax.ppermute(x, 'expert', [(i, i ^ offset) for i in range(n)])]
    another operation x4 -> x2, other arithmetic: 1.5 us -> 0.14 us
  transfers between devices with their start and end apart: 20 -> 20, of which waited for: 15 -> 17; matrix products, arithmetic and copies ran while one was open for 7% -> 0% of each run, Pallas kernels for 0% -> 5%
where the time goes in v2:
time: 86.4 us; the launch traced here: 86.2 us
  waiting for transfers between devices  44.8 us (52%)
  starting transfers between devices  25.9 us (30%)
  Pallas kernels  12.9 us (15%)
  other arithmetic  1.33 us (2%)
  between operations  0.89 us (1%)
    ppermute x20, waiting for transfers between devices, swap(): return lax.ppermute(x, 'expert', [(i, i ^ offset) for i in range(n)])  44.8 us
    ppermute x20, starting transfers between devices, swap(): return lax.ppermute(x, 'expert', [(i, i ^ offset) for i in range(n)])  25.9 us
    pallas_call x2, Pallas kernels, run_ffn(): pl.pallas_call(functools.partial(ffn_kernel, step), out_shape=(jax.ShapeD...  7.16 us
    pallas_call x1, Pallas kernels, run_load(): pl.pallas_call(load_kernel, out_shape=tuple((jax.ShapeDtypeStruct(w.shape...  3.79 us
  transfers between devices with their start and end apart: 20, of which 17 were waited for; matrix products, arithmetic and copies ran while one was open for 0% of the time, Pallas kernels for 5%

profile of v2, /device:TPU:0, one launch (start us, length us, event | category | flops | bytes accessed | tf_op | source)
XLA Modules:
  0.0 86.2 jit_solution(17283055608091763961)
XLA Ops:
  1.7 3.1 %collective-permute-start = (bf16[16,2176]{1,0:T(8,128)(2,1)S(1)}, bf16[16,2176]{1,0:T(8,128)(2,1)S(1)}, u32[]{:S(2)}, u32[]{:S(2)}) collective-permute-start(bf16[16,2176]{1,0:T(8,128)(2,1)S(1)} %open_rows.1), channel_id=1, source_target_pairs={{0,4},{1,5},{2,6},{3,7},{4,0},{5,1},{6,2},{7,3},{8,12},{9,13},{10,... | collective-permute-start | bytes 208904 | tf_op jit(solution)/shard_map/ppermute | solution.py:299
  4.8 2.6 %collective-permute-start.1 = (bf16[16,2176]{1,0:T(8,128)(2,1)S(1)}, bf16[16,2176]{1,0:T(8,128)(2,1)S(1)}, u32[]{:S(2)}, u32[]{:S(2)}) collective-permute-start(bf16[16,2176]{1,0:T(8,128)(2,1)S(1)} %open_rows.1), channel_id=1, source_target_pairs={{0,8},{1,9},{2,10},{3,11},{4,12},{5,13},{6,14},{7,15},{8,0},{9,1},... | collective-permute-start | bytes 208904 | tf_op jit(solution)/shard_map/ppermute | solution.py:299
  7.4 3.8 %load_weights.1 = (bf16[1,2048,768]{2,1,0:T(8,128)(2,1)S(1)}, bf16[1,2048,768]{2,1,0:T(8,128)(2,1)S(1)}, bf16[1,768,2048]{2,1,0:T(8,128)(2,1)S(1)}) custom-call(bf16[1,2048,768]{2,1,0:T(8,128)(2,1)} %refs_0_.2, bf16[1,2048,768]{2,1,0:T(8,128)(2,1)} %refs_1_.2, bf16[1,768,2048]{2,1,0:T(8,128)(2,1)} %refs_2_), custom_call_target="tpu_custom_call" | custom-call | bytes 18874368 | tf_op jit(solution)/shard_map/load_weights/pallas_call | solution.py:177
  13.7 1.6 %collective-permute-start.3 = (bf16[64,2176]{1,0:T(8,128)(2,1)S(1)}, bf16[64,2176]{1,0:T(8,128)(2,1)S(1)}, u32[]{:S(2)}, u32[]{:S(2)}) collective-permute-start(bf16[64,2176]{1,0:T(8,128)(2,1)S(1)} %pad_maximum_fusion), channel_id=1, source_target_pairs={{0,2},{1,3},{2,0},{3,1},{4,6},{5,7},{6,4},{7,5},{8,10},{9,11},{10,... | collective-permute-start | bytes 835592 | tf_op jit(solution)/shard_map/ppermute | solution.py:299
  15.3 5.0 %collective-permute-done.3 = bf16[64,2176]{1,0:T(8,128)(2,1)S(1)} collective-permute-done((bf16[64,2176]{1,0:T(8,128)(2,1)S(1)}, bf16[64,2176]{1,0:T(8,128)(2,1)S(1)}, u32[]{:S(2)}, u32[]{:S(2)}) %collective-permute-start.3) | collective-permute-done | bytes 278560 | tf_op jit(solution)/shard_map/ppermute | solution.py:299
  20.5 1.9 %collective-permute-done.4 = bf16[128,2176]{1,0:T(8,128)(2,1)S(1)} collective-permute-done((bf16[128,2176]{1,0:T(8,128)(2,1)S(1)}, bf16[128,2176]{1,0:T(8,128)(2,1)S(1)}, u32[]{:S(2)}, u32[]{:S(2)}) %collective-permute-start.4) | collective-permute-done | bytes 557088 | tf_op jit(solution)/shard_map/ppermute | solution.py:299
  22.5 3.6 %ffn0.1 = (f32[128,2048]{1,0:T(8,128)S(1)}, bf16[128,2048]{1,0:T(8,128)(2,1)S(1)}) custom-call(bf16[256,2176]{1,0:T(8,128)(2,1)S(1)} %constant_dynamic-update-slice_fusion.5.x_ref.meta_ref, bf16[256,2176]{1,0:T(8,128)(2,1)S(1)} %constant_dynamic-update-slice_fusion.5.x_ref.meta_ref, bf16[16,2048]{1,0:T(8,128)(2,1)S(1)} %bitcast.4, ...), custom_call_target="tpu_custom_call" | custom-call | flops 2415919104 | bytes 2097152 | tf_op jit(solution)/shard_map/ffn0/pallas_call | solution.py:267
  26.3 1.8 %collective-permute-done.5 = bf16[128,2048]{1,0:T(8,128)(2,1)S(1)} collective-permute-done((bf16[128,2048]{1,0:T(8,128)(2,1)S(1)}, bf16[128,2048]{1,0:T(8,128)(2,1)S(1)}, u32[]{:S(2)}, u32[]{:S(2)}) %collective-permute-start.5) | collective-permute-done | bytes 524320 | tf_op jit(solution)/shard_map/ppermute | solution.py:299
  29.8 6.8 %collective-permute-done.6 = bf16[64,2048]{1,0:T(8,128)(2,1)S(1)} collective-permute-done((bf16[64,2048]{1,0:T(8,128)(2,1)S(1)}, bf16[64,2048]{1,0:T(8,128)(2,1)S(1)}, u32[]{:S(2)}, u32[]{:S(2)}) %collective-permute-start.6) | collective-permute-done | bytes 262176 | tf_op jit(solution)/shard_map/ppermute | solution.py:299
  36.7 2.5 %collective-permute-start.9 = (bf16[16,2048]{1,0:T(8,128)(2,1)S(1)}, bf16[16,2048]{1,0:T(8,128)(2,1)S(1)}, u32[]{:S(2)}, u32[]{:S(2)}) collective-permute-start(bf16[16,2048]{1,0:T(8,128)(2,1)S(1)} %get-tuple-element.66), channel_id=1, source_target_pairs={{0,12},{1,13},{2,14},{3,15},{4,8},{5,9},{6,10},{7,11},{8,4},{9,5},... | collective-permute-start | bytes 196616 | tf_op jit(solution)/shard_map/ppermute | solution.py:299
  39.4 1.8 %collective-permute-start.7 = (bf16[16,2048]{1,0:T(8,128)(2,1)S(1)}, bf16[16,2048]{1,0:T(8,128)(2,1)S(1)}, u32[]{:S(2)}, u32[]{:S(2)}) collective-permute-start(bf16[16,2048]{1,0:T(8,128)(2,1)S(1)} %get-tuple-element.65), channel_id=1, source_target_pairs={{0,4},{1,5},{2,6},{3,7},{4,0},{5,1},{6,2},{7,3},{8,12},{9,13},{10,... | collective-permute-start | bytes 196616 | tf_op jit(solution)/shard_map/ppermute | solution.py:299
  41.2 2.4 %collective-permute-done.9 = bf16[16,2048]{1,0:T(8,128)(2,1)S(1)} collective-permute-done((bf16[16,2048]{1,0:T(8,128)(2,1)S(1)}, bf16[16,2048]{1,0:T(8,128)(2,1)S(1)}, u32[]{:S(2)}, u32[]{:S(2)}) %collective-permute-start.9) | collective-permute-done | bytes 65568 | tf_op jit(solution)/shard_map/ppermute | solution.py:299
  43.5 1.8 %collective-permute-done.8 = bf16[16,2048]{1,0:T(8,128)(2,1)S(1)} collective-permute-done((bf16[16,2048]{1,0:T(8,128)(2,1)S(1)}, bf16[16,2048]{1,0:T(8,128)(2,1)S(1)}, u32[]{:S(2)}, u32[]{:S(2)}) %collective-permute-start.8) | collective-permute-done | bytes 65568 | tf_op jit(solution)/shard_map/ppermute | solution.py:299
  45.8 2.9 %collective-permute-start.11 = (bf16[16,2048]{1,0:T(8,128)(2,1)S(1)}, bf16[16,2048]{1,0:T(8,128)(2,1)S(1)}, u32[]{:S(2)}, u32[]{:S(2)}) collective-permute-start(bf16[16,2048]{1,0:T(8,128)(2,1)S(1)} %fusion.2), channel_id=1, source_target_pairs={{0,8},{1,9},{2,10},{3,11},{4,12},{5,13},{6,14},{7,15},{8,0},{9,1},... | collective-permute-start | bytes 196616 | tf_op jit(solution)/shard_map/ppermute | solution.py:299
  50.4 2.8 %collective-permute-done.11 = bf16[16,2048]{1,0:T(8,128)(2,1)S(1)} collective-permute-done((bf16[16,2048]{1,0:T(8,128)(2,1)S(1)}, bf16[16,2048]{1,0:T(8,128)(2,1)S(1)}, u32[]{:S(2)}, u32[]{:S(2)}) %collective-permute-start.11) | collective-permute-done | bytes 65568 | tf_op jit(solution)/shard_map/ppermute | solution.py:299
  53.2 1.6 %collective-permute-done.12 = bf16[16,2048]{1,0:T(8,128)(2,1)S(1)} collective-permute-done((bf16[16,2048]{1,0:T(8,128)(2,1)S(1)}, bf16[16,2048]{1,0:T(8,128)(2,1)S(1)}, u32[]{:S(2)}, u32[]{:S(2)}) %collective-permute-start.12) | collective-permute-done | bytes 65568 | tf_op jit(solution)/shard_map/ppermute | solution.py:299
  54.8 1.6 %collective-permute-start.13 = (bf16[64,2048]{1,0:T(8,128)(2,1)S(1)}, bf16[64,2048]{1,0:T(8,128)(2,1)S(1)}, u32[]{:S(2)}, u32[]{:S(2)}) collective-permute-start(bf16[64,2048]{1,0:T(8,128)(2,1)S(1)} %pad_maximum_fusion.1), channel_id=1, source_target_pairs={{0,2},{1,3},{2,0},{3,1},{4,6},{5,7},{6,4},{7,5},{8,10},{9,11},{10,... | collective-permute-start | bytes 786440 | tf_op jit(solution)/shard_map/ppermute | solution.py:299
  56.5 4.8 %collective-permute-done.13 = bf16[64,2048]{1,0:T(8,128)(2,1)S(1)} collective-permute-done((bf16[64,2048]{1,0:T(8,128)(2,1)S(1)}, bf16[64,2048]{1,0:T(8,128)(2,1)S(1)}, u32[]{:S(2)}, u32[]{:S(2)}) %collective-permute-start.13) | collective-permute-done | bytes 262176 | tf_op jit(solution)/shard_map/ppermute | solution.py:299
  61.4 1.9 %collective-permute-done.14 = bf16[128,2048]{1,0:T(8,128)(2,1)S(1)} collective-permute-done((bf16[128,2048]{1,0:T(8,128)(2,1)S(1)}, bf16[128,2048]{1,0:T(8,128)(2,1)S(1)}, u32[]{:S(2)}, u32[]{:S(2)}) %collective-permute-start.14) | collective-permute-done | bytes 524320 | tf_op jit(solution)/shard_map/ppermute | solution.py:299
  63.3 3.6 %ffn1.1 = (f32[128,2048]{1,0:T(8,128)S(1)}, bf16[128,2048]{1,0:T(8,128)(2,1)S(1)}) custom-call(bf16[256,2048]{1,0:T(8,128)(2,1)S(1)} %constant_dynamic-update-slice_fusion.16.x_ref, bf16[256,2176]{1,0:T(8,128)(2,1)S(1)} %constant_dynamic-update-slice_fusion.5.x_ref.meta_ref, bf16[16,2048]{1,0:T(8,128)(2,1)S(1)} %bitcast.5, ...), custom_call_target="tpu_custom_call" | custom-call | flops 2415919104 | bytes 2097152 | tf_op jit(solution)/shard_map/ffn1/pallas_call | solution.py:267
  67.1 1.8 %collective-permute-done.15 = bf16[128,2048]{1,0:T(8,128)(2,1)S(1)} collective-permute-done((bf16[128,2048]{1,0:T(8,128)(2,1)S(1)}, bf16[128,2048]{1,0:T(8,128)(2,1)S(1)}, u32[]{:S(2)}, u32[]{:S(2)}) %collective-permute-start.15) | collective-permute-done | bytes 524320 | tf_op jit(solution)/shard_map/ppermute | solution.py:299
  70.7 6.8 %collective-permute-done.16 = bf16[64,2048]{1,0:T(8,128)(2,1)S(1)} collective-permute-done((bf16[64,2048]{1,0:T(8,128)(2,1)S(1)}, bf16[64,2048]{1,0:T(8,128)(2,1)S(1)}, u32[]{:S(2)}, u32[]{:S(2)}) %collective-permute-start.16) | collective-permute-done | bytes 262176 | tf_op jit(solution)/shard_map/ppermute | solution.py:299
  77.6 1.6 %collective-permute-start.19 = (bf16[16,2048]{1,0:T(8,128)(2,1)S(1)}, bf16[16,2048]{1,0:T(8,128)(2,1)S(1)}, u32[]{:S(2)}, u32[]{:S(2)}) collective-permute-start(bf16[16,2048]{1,0:T(8,128)(2,1)S(1)} %get-tuple-element.61), channel_id=1, source_target_pairs={{0,12},{1,13},{2,14},{3,15},{4,8},{5,9},{6,10},{7,11},{8,4},{9,5},... | collective-permute-start | bytes 196616 | tf_op jit(solution)/shard_map/ppermute | solution.py:299
  79.2 2.8 %collective-permute-start.17 = (bf16[16,2048]{1,0:T(8,128)(2,1)S(1)}, bf16[16,2048]{1,0:T(8,128)(2,1)S(1)}, u32[]{:S(2)}, u32[]{:S(2)}) collective-permute-start(bf16[16,2048]{1,0:T(8,128)(2,1)S(1)} %get-tuple-element.60), channel_id=1, source_target_pairs={{0,4},{1,5},{2,6},{3,7},{4,0},{5,1},{6,2},{7,3},{8,12},{9,13},{10,... | collective-permute-start | bytes 196616 | tf_op jit(solution)/shard_map/ppermute | solution.py:299
  (56 shorter events, 14.4 us)
Async XLA Ops:
  1.7 9.5 %collective-permute-start = (bf16[16,2176]{1,0:T(8,128)(2,1)S(1)}, bf16[16,2176]{1,0:T(8,128)(2,1)S(1)}, u32[]{:S(2)}, u32[]{:S(2)}) collective-permute-start(bf16[16,2176]{1,0:T(8,128)(2,1)S(1)} %open_rows.1), channel_id=1, source_target_pairs={{0,4},{1,5},{2,6},{3,7},{4,0},{5,1},{6,2},{7,3},{8,12},{9,13},{10,... | collective-permute-start | bytes 208904 | tf_op jit(solution)/shard_map/ppermute | solution.py:299
  4.8 7.5 %collective-permute-start.1 = (bf16[16,2176]{1,0:T(8,128)(2,1)S(1)}, bf16[16,2176]{1,0:T(8,128)(2,1)S(1)}, u32[]{:S(2)}, u32[]{:S(2)}) collective-permute-start(bf16[16,2176]{1,0:T(8,128)(2,1)S(1)} %open_rows.1), channel_id=1, source_target_pairs={{0,8},{1,9},{2,10},{3,11},{4,12},{5,13},{6,14},{7,15},{8,0},{9,1},... | collective-permute-start | bytes 208904 | tf_op jit(solution)/shard_map/ppermute | solution.py:299
  7.4 6.2 %collective-permute-start.2 = (bf16[16,2176]{1,0:T(8,128)(2,1)S(1)}, bf16[16,2176]{1,0:T(8,128)(2,1)S(1)}, u32[]{:S(2)}, u32[]{:S(2)}) collective-permute-start(bf16[16,2176]{1,0:T(8,128)(2,1)S(1)} %open_rows.1), channel_id=1, source_target_pairs={{0,12},{1,13},{2,14},{3,15},{4,8},{5,9},{6,10},{7,11},{8,4},{9,5},... | collective-permute-start | bytes 208904 | tf_op jit(solution)/shard_map/ppermute | solution.py:299
  13.7 6.7 %collective-permute-start.3 = (bf16[64,2176]{1,0:T(8,128)(2,1)S(1)}, bf16[64,2176]{1,0:T(8,128)(2,1)S(1)}, u32[]{:S(2)}, u32[]{:S(2)}) collective-permute-start(bf16[64,2176]{1,0:T(8,128)(2,1)S(1)} %pad_maximum_fusion), channel_id=1, source_target_pairs={{0,2},{1,3},{2,0},{3,1},{4,6},{5,7},{6,4},{7,5},{8,10},{9,11},{10,... | collective-permute-start | bytes 835592 | tf_op jit(solution)/shard_map/ppermute | solution.py:299
  15.3 7.2 %copy-start = (bf16[2048,16]{0,1:T(8,128)(2,1)S(1)}, bf16[2048,16]{0,1:T(8,128)(2,1)}, u32[]{:S(2)}) copy-start(bf16[2048,16]{0,1:T(8,128)(2,1)} %param.14) | copy-start | bytes 196612
  20.4 2.0 %collective-permute-start.4 = (bf16[128,2176]{1,0:T(8,128)(2,1)S(1)}, bf16[128,2176]{1,0:T(8,128)(2,1)S(1)}, u32[]{:S(2)}, u32[]{:S(2)}) collective-permute-start(bf16[128,2176]{1,0:T(8,128)(2,1)S(1)} %get-tuple-element.58), channel_id=1, source_target_pairs={{0,1},{1,0},{2,3},{3,2},{4,5},{5,4},{6,7},{7,6},{8,9},{9,8},{10,11... | collective-permute-start | bytes 1671176 | tf_op jit(solution)/shard_map/ppermute | solution.py:299
  26.1 2.0 %collective-permute-start.5 = (bf16[128,2048]{1,0:T(8,128)(2,1)S(1)}, bf16[128,2048]{1,0:T(8,128)(2,1)S(1)}, u32[]{:S(2)}, u32[]{:S(2)}) collective-permute-start(bf16[128,2048]{1,0:T(8,128)(2,1)S(1)} %get-tuple-element.42), channel_id=1, source_target_pairs={{0,1},{1,0},{2,3},{3,2},{4,5},{5,4},{6,7},{7,6},{8,9},{9,8},{10,11... | collective-permute-start | bytes 1572872 | tf_op jit(solution)/shard_map/ppermute | solution.py:299
  28.2 13.0 %copy-start.3 = (bf16[2048]{0:T(1024)(128)(2,1)S(1)}, bf16[2048]{0:T(1024)(128)(2,1)}, u32[]{:S(2)}) copy-start(bf16[2048]{0:T(1024)(128)(2,1)} %refs_1_.1) | copy-start | bytes 12292
  28.2 17.2 %copy-start.2 = (bf16[16,2048]{1,0:T(8,128)(2,1)S(1)}, bf16[16,2048]{1,0:T(8,128)(2,1)}, u32[]{:S(2)}) copy-start(bf16[16,2048]{1,0:T(8,128)(2,1)} %refs_0_.1) | copy-start | bytes 196612
  28.2 8.4 %collective-permute-start.6 = (bf16[64,2048]{1,0:T(8,128)(2,1)S(1)}, bf16[64,2048]{1,0:T(8,128)(2,1)S(1)}, u32[]{:S(2)}, u32[]{:S(2)}) collective-permute-start(bf16[64,2048]{1,0:T(8,128)(2,1)S(1)} %slice.89), channel_id=1, source_target_pairs={{0,2},{1,3},{2,0},{3,1},{4,6},{5,7},{6,4},{7,5},{8,10},{9,11},{10,... | collective-permute-start | bytes 786440 | tf_op jit(solution)/shard_map/ppermute | solution.py:299
  36.7 6.8 %collective-permute-start.9 = (bf16[16,2048]{1,0:T(8,128)(2,1)S(1)}, bf16[16,2048]{1,0:T(8,128)(2,1)S(1)}, u32[]{:S(2)}, u32[]{:S(2)}) collective-permute-start(bf16[16,2048]{1,0:T(8,128)(2,1)S(1)} %get-tuple-element.66), channel_id=1, source_target_pairs={{0,12},{1,13},{2,14},{3,15},{4,8},{5,9},{6,10},{7,11},{8,4},{9,5},... | collective-permute-start | bytes 196616 | tf_op jit(solution)/shard_map/ppermute | solution.py:299
  39.2 6.2 %collective-permute-start.8 = (bf16[16,2048]{1,0:T(8,128)(2,1)S(1)}, bf16[16,2048]{1,0:T(8,128)(2,1)S(1)}, u32[]{:S(2)}, u32[]{:S(2)}) collective-permute-start(bf16[16,2048]{1,0:T(8,128)(2,1)S(1)} %get-tuple-element.67), channel_id=1, source_target_pairs={{0,8},{1,9},{2,10},{3,11},{4,12},{5,13},{6,14},{7,15},{8,0},{9,1},... | collective-permute-start | bytes 196616 | tf_op jit(solution)/shard_map/ppermute | solution.py:299
  39.4 6.0 %collective-permute-start.7 = (bf16[16,2048]{1,0:T(8,128)(2,1)S(1)}, bf16[16,2048]{1,0:T(8,128)(2,1)S(1)}, u32[]{:S(2)}, u32[]{:S(2)}) collective-permute-start(bf16[16,2048]{1,0:T(8,128)(2,1)S(1)} %get-tuple-element.65), channel_id=1, source_target_pairs={{0,4},{1,5},{2,6},{3,7},{4,0},{5,1},{6,2},{7,3},{8,12},{9,13},{10,... | collective-permute-start | bytes 196616 | tf_op jit(solution)/shard_map/ppermute | solution.py:299
  45.7 4.8 %collective-permute-start.10 = (bf16[16,2048]{1,0:T(8,128)(2,1)S(1)}, bf16[16,2048]{1,0:T(8,128)(2,1)S(1)}, u32[]{:S(2)}, u32[]{:S(2)}) collective-permute-start(bf16[16,2048]{1,0:T(8,128)(2,1)S(1)} %fusion.2), channel_id=1, source_target_pairs={{0,4},{1,5},{2,6},{3,7},{4,0},{5,1},{6,2},{7,3},{8,12},{9,13},{10,... | collective-permute-start | bytes 196616 | tf_op jit(solution)/shard_map/ppermute | solution.py:299
  45.8 7.4 %collective-permute-start.11 = (bf16[16,2048]{1,0:T(8,128)(2,1)S(1)}, bf16[16,2048]{1,0:T(8,128)(2,1)S(1)}, u32[]{:S(2)}, u32[]{:S(2)}) collective-permute-start(bf16[16,2048]{1,0:T(8,128)(2,1)S(1)} %fusion.2), channel_id=1, source_target_pairs={{0,8},{1,9},{2,10},{3,11},{4,12},{5,13},{6,14},{7,15},{8,0},{9,1},... | collective-permute-start | bytes 196616 | tf_op jit(solution)/shard_map/ppermute | solution.py:299
  48.7 6.1 %collective-permute-start.12 = (bf16[16,2048]{1,0:T(8,128)(2,1)S(1)}, bf16[16,2048]{1,0:T(8,128)(2,1)S(1)}, u32[]{:S(2)}, u32[]{:S(2)}) collective-permute-start(bf16[16,2048]{1,0:T(8,128)(2,1)S(1)} %fusion.2), channel_id=1, source_target_pairs={{0,12},{1,13},{2,14},{3,15},{4,8},{5,9},{6,10},{7,11},{8,4},{9,5},... | collective-permute-start | bytes 196616 | tf_op jit(solution)/shard_map/ppermute | solution.py:299
  54.8 6.4 %collective-permute-start.13 = (bf16[64,2048]{1,0:T(8,128)(2,1)S(1)}, bf16[64,2048]{1,0:T(8,128)(2,1)S(1)}, u32[]{:S(2)}, u32[]{:S(2)}) collective-permute-start(bf16[64,2048]{1,0:T(8,128)(2,1)S(1)} %pad_maximum_fusion.1), channel_id=1, source_target_pairs={{0,2},{1,3},{2,0},{3,1},{4,6},{5,7},{6,4},{7,5},{8,10},{9,11},{10,... | collective-permute-start | bytes 786440 | tf_op jit(solution)/shard_map/ppermute | solution.py:299
  61.3 2.0 %collective-permute-start.14 = (bf16[128,2048]{1,0:T(8,128)(2,1)S(1)}, bf16[128,2048]{1,0:T(8,128)(2,1)S(1)}, u32[]{:S(2)}, u32[]{:S(2)}) collective-permute-start(bf16[128,2048]{1,0:T(8,128)(2,1)S(1)} %get-tuple-element.63), channel_id=1, source_target_pairs={{0,1},{1,0},{2,3},{3,2},{4,5},{5,4},{6,7},{7,6},{8,9},{9,8},{10,11... | collective-permute-start | bytes 1572872 | tf_op jit(solution)/shard_map/ppermute | solution.py:299
  66.9 2.0 %collective-permute-start.15 = (bf16[128,2048]{1,0:T(8,128)(2,1)S(1)}, bf16[128,2048]{1,0:T(8,128)(2,1)S(1)}, u32[]{:S(2)}, u32[]{:S(2)}) collective-permute-start(bf16[128,2048]{1,0:T(8,128)(2,1)S(1)} %get-tuple-element.51), channel_id=1, source_target_pairs={{0,1},{1,0},{2,3},{3,2},{4,5},{5,4},{6,7},{7,6},{8,9},{9,8},{10,11... | collective-permute-start | bytes 1572872 | tf_op jit(solution)/shard_map/ppermute | solution.py:299
  69.1 13.0 %copy-start.1 = (s32[16]{0:T(128)S(1)}, s32[16]{0:T(128)}, u32[]{:S(2)}) copy-start(s32[16]{0:T(128)} %param.18) | copy-start | bytes 196
  69.1 8.4 %collective-permute-start.16 = (bf16[64,2048]{1,0:T(8,128)(2,1)S(1)}, bf16[64,2048]{1,0:T(8,128)(2,1)S(1)}, u32[]{:S(2)}, u32[]{:S(2)}) collective-permute-start(bf16[64,2048]{1,0:T(8,128)(2,1)S(1)} %slice.88), channel_id=1, source_target_pairs={{0,2},{1,3},{2,0},{3,1},{4,6},{5,7},{6,4},{7,5},{8,10},{9,11},{10,... | collective-permute-start | bytes 786440 | tf_op jit(solution)/shard_map/ppermute | solution.py:299
  77.6 6.7 %collective-permute-start.19 = (bf16[16,2048]{1,0:T(8,128)(2,1)S(1)}, bf16[16,2048]{1,0:T(8,128)(2,1)S(1)}, u32[]{:S(2)}, u32[]{:S(2)}) collective-permute-start(bf16[16,2048]{1,0:T(8,128)(2,1)S(1)} %get-tuple-element.61), channel_id=1, source_target_pairs={{0,12},{1,13},{2,14},{3,15},{4,8},{5,9},{6,10},{7,11},{8,4},{9,5},... | collective-permute-start | bytes 196616 | tf_op jit(solution)/shard_map/ppermute | solution.py:299
  79.2 6.3 %collective-permute-start.18 = (bf16[16,2048]{1,0:T(8,128)(2,1)S(1)}, bf16[16,2048]{1,0:T(8,128)(2,1)S(1)}, u32[]{:S(2)}, u32[]{:S(2)}) collective-permute-start(bf16[16,2048]{1,0:T(8,128)(2,1)S(1)} %get-tuple-element.62), channel_id=1, source_target_pairs={{0,8},{1,9},{2,10},{3,11},{4,12},{5,13},{6,14},{7,15},{8,0},{9,1},... | collective-permute-start | bytes 196616 | tf_op jit(solution)/shard_map/ppermute | solution.py:299
  79.2 6.3 %collective-permute-start.17 = (bf16[16,2048]{1,0:T(8,128)(2,1)S(1)}, bf16[16,2048]{1,0:T(8,128)(2,1)S(1)}, u32[]{:S(2)}, u32[]{:S(2)}) collective-permute-start(bf16[16,2048]{1,0:T(8,128)(2,1)S(1)} %get-tuple-element.60), channel_id=1, source_target_pairs={{0,4},{1,5},{2,6},{3,7},{4,0},{5,1},{6,2},{7,3},{8,12},{9,13},{10,... | collective-permute-start | bytes 196616 | tf_op jit(solution)/shard_map/ppermute | solution.py:299
